TPU v7x, 512 devices: a whole 4x8x8 slice. The times are simulated.
512 devices in a mesh: segment: 32 (over y_lo, z), dp: 8 (over x, core), seq: 2 (over y_hi).
Axes of the slice: x: 4, y: 8 (y_hi: 2, y_lo: 4; y = y_hi * 4 + y_lo), z: 8, core: 2. Of those that a mesh axis runs over, the one named last changes fastest.
Arguments:
- stored_part_activation: bfloat16 [32, 2, 8, 256, 2048], P('segment', None, 'dp', 'seq'), may hold values from -64 to 64
- pending_sensitivity: bfloat16 [32, 8, 256, 2048], P('segment', 'dp', 'seq'), may hold values from -0.119628906 to 0.119628906
- uppermost_result_derivative: bfloat16 [1, 8, 256, 2048], P(None, 'dp', 'seq'), may hold values from -0.119628906 to 0.119628906
- scaling_factors: float32 [32, 4, 2048], P('segment'), may hold values from -0.5 to 5
- attended_tile_table: int32 [32, 2, 8, 2, 2], P('segment', None, 'dp'), may hold values from 0 to 1, as said below
- active_tile_number: int32 [32, 2, 8, 2], P('segment', None, 'dp'), may hold values from 1 to 2
Outputs:
- factor_derivatives: float32 [32, 4, 2048], P('segment')
Inputs may be any that keep to these rules, and one draw needn't show every extreme that they name: `attended_tile_table`: each list names every key block of its sample once; the allowed ones come first.
All inputs are finite; a program needn't handle non-finite values.
Results may differ from a plain program's by a relative error of at most 0.009.
Values may be sent and summed in bfloat16 or wider, within the bound.
A program may use at most 64 MiB of HBM per device.

v0:
```python
import jax
import jax.numpy as jnp
from jax import lax
from jax.sharding import PartitionSpec as P

HEAD_DIM = 128
BLK = 128


epsilon = 1e-06


def partner(block, axis, apart):
    count = lax.axis_size(axis)
    route = []
    for low in range(count):
        high = low | 1 << apart
        if high != low and high < count:
            route += [(low, high), (high, low)]
    return lax.ppermute(block, axis, route)


def from_behind(block, axis, distance):
    devices = range(lax.axis_size(axis))
    route = [(i - distance, i) for i in devices if i - distance in devices]
    return lax.ppermute(block, axis, route)


def normed_of(inputs):
    widened = inputs.astype(jnp.float32).reshape(
        inputs.shape[:-1] + (inputs.shape[-1] // HEAD_DIM, HEAD_DIM)
    )
    inv_rms = lax.rsqrt(jnp.mean(widened * widened, axis=-1, keepdims=True) + epsilon)
    return (widened * inv_rms, inv_rms)


def norm_back(grad_norm, norm_val, inv_rms):
    return inv_rms * (grad_norm - norm_val * jnp.mean(grad_norm * norm_val, axis=-1, keepdims=True))


def allowed_blocks(block_list, live_count):
    block_total = block_list.shape[0]
    live_slots = jnp.arange(block_total)[None, :] < live_count[:, None]
    matches = (block_list[:, :, None] == jnp.arange(block_total)[None, None, :]) & live_slots[
        :, :, None
    ]
    return jnp.any(matches, axis=1)


def token_mask(permitted, query_half, seq_index, dev_blocks):
    local_blocks = jnp.arange(dev_blocks, dtype=jnp.int32)
    query_rows = query_half * dev_blocks + local_blocks
    key_order = jnp.concatenate(
        [seq_index * dev_blocks + local_blocks, (1 - seq_index) * dev_blocks + local_blocks]
    )
    picked = permitted[query_rows[:, None], key_order[None, :]]
    return jnp.repeat(jnp.repeat(picked, BLK, axis=0), BLK, axis=1)


def attend(query_norm, key_norm, gain_heads, allowed, incoming, scaling):
    queries = (query_norm * gain_heads[0]).astype(jnp.bfloat16)
    key_mat = (key_norm * gain_heads[1]).astype(jnp.bfloat16)
    val_mat = (key_norm * gain_heads[2]).astype(jnp.bfloat16)
    scores = (
        jnp.einsum("thd,shd->hts", queries, key_mat, preferred_element_type=jnp.float32) * scaling
    )
    scores = jnp.where(allowed[None], scores, -jnp.inf)
    exped = jnp.exp(scores - jnp.max(scores, axis=-1, keepdims=True))
    probs = exped / jnp.sum(exped, axis=-1, keepdims=True)
    probs_low = probs.astype(jnp.bfloat16)
    output = jnp.einsum("hts,shd->thd", probs_low, val_mat, preferred_element_type=jnp.float32)
    grad_out = (gain_heads[3] * incoming).astype(jnp.bfloat16)
    grad_probs = jnp.einsum("thd,shd->hts", grad_out, val_mat, preferred_element_type=jnp.float32)
    grad_scores = (
        probs * (grad_probs - jnp.sum(probs * grad_probs, axis=-1, keepdims=True))
    ).astype(jnp.bfloat16)
    return (queries, key_mat, probs_low, output, grad_out, grad_scores)


def shards(
    stored_part_activation,
    pending_sensitivity,
    uppermost_result_derivative,
    scaling_factors,
    attended_tile_table,
    active_tile_number,
):
    segments = lax.axis_size("segment")
    segment_index = lax.axis_index("segment")
    seq_index = lax.axis_index("seq")
    window = stored_part_activation.shape[1]
    row_count = stored_part_activation.shape[3]
    channels = stored_part_activation.shape[4]
    head_count = channels // HEAD_DIM
    dev_blocks = row_count // BLK
    scaling = HEAD_DIM ** (-0.5)
    own_window = stored_part_activation[0, :, 0]
    gain_heads = scaling_factors[0].reshape(4, head_count, HEAD_DIM)
    incoming_sensitivity = pending_sensitivity[0, 0].astype(jnp.float32)
    totals = jnp.zeros((4, head_count, HEAD_DIM), jnp.float32)
    for step_index in range(window):
        own_rows = own_window[step_index]
        other_rows = partner(own_rows, "seq", 0)
        permitted = allowed_blocks(
            attended_tile_table[0, step_index, 0], active_tile_number[0, step_index, 0]
        )
        own_norm, own_inv = normed_of(own_rows)
        other_norm, other_inv = normed_of(other_rows)
        key_norm = jnp.concatenate([own_norm, other_norm], axis=0)
        incoming = incoming_sensitivity.reshape(row_count, head_count, HEAD_DIM)
        own_allowed = token_mask(permitted, seq_index, seq_index, dev_blocks)
        queries, key_mat, probs_low, output, grad_out, grad_scores = attend(
            own_norm, key_norm, gain_heads, own_allowed, incoming, scaling
        )
        grad_query = (
            jnp.einsum("hts,shd->thd", grad_scores, key_mat, preferred_element_type=jnp.float32)
            * scaling
        )
        grad_key = (
            jnp.einsum("hts,thd->shd", grad_scores, queries, preferred_element_type=jnp.float32)
            * scaling
        )
        grad_value = jnp.einsum(
            "hts,thd->shd", probs_low, grad_out, preferred_element_type=jnp.float32
        )
        key_part = grad_key * gain_heads[1] + grad_value * gain_heads[2]
        self_part = key_part[:row_count]
        key_terms = jnp.sum(grad_key * key_norm, axis=0)
        value_terms = jnp.sum(grad_value * key_norm, axis=0)
        if step_index < window - 1:
            lent = norm_back(key_part[row_count:], other_norm, other_inv).astype(jnp.bfloat16)
            returned = partner(lent, "seq", 0).astype(jnp.float32)
        grad_terms = jnp.stack(
            [
                jnp.sum(grad_query * own_norm, axis=0),
                key_terms,
                value_terms,
                jnp.sum(output * incoming, axis=0),
            ]
        )
        totals = totals + grad_terms
        if step_index < window - 1:
            grad_input = (
                incoming
                + norm_back(grad_query * gain_heads[0] + self_part, own_norm, own_inv)
                + returned
            )
            received = from_behind(grad_input.reshape(row_count, channels), "segment", -1)
            incoming_sensitivity = jnp.where(
                segment_index == segments - 1,
                uppermost_result_derivative[step_index, 0].astype(jnp.float32),
                received,
            )
    summed = lax.psum(totals.reshape(4, channels), ("dp", "seq"))
    return summed[None]


def solution(mesh):
    placed = (
        P("segment", None, "dp", "seq", None),
        P("segment", "dp", "seq", None),
        P(None, "dp", "seq", None),
        P("segment", None, None),
        P("segment", None, "dp", None, None),
        P("segment", None, "dp", None),
    )
    return jax.shard_map(
        shards, mesh=mesh, in_specs=placed, out_specs=P("segment", None, None), check_vma=False
    )
```

profile of v0, /device:TPU:24, one launch (start us, length us, event | category | flops | bytes accessed | tf_op | source)
XLA Modules:
  0.0 220.2 jit_solution(2187491883206557950)
XLA Ops:
  0.0 2.7 %slice_convert_fusion = (f32[1,1,1,128,2048]{4,3,2,1,0:T(8,128)}, bf16[128,2048]{1,0:T(8,128)(2,1)}, bf16[128,2048]{1,0:T(8,128)(2,1)}, f32[1,1,1,128,2048]{4,3,2,1,0:T(8,128)S(1)}) fusion(bf16[1,2,1,128,2048]{4,3,2,1,0:T(8,128)(2,1)} %param.6), kind=kLoop, calls=%fused_computation.75 | loop fusion | flops 524288 | bytes 4194304 | tf_op jit(solution)/shard_map/convert_element_type | solution.py:30
  2.7 5.0 %collective-permute-start = (bf16[128,2048]{1,0:T(8,128)(2,1)}, bf16[128,2048]{1,0:T(8,128)(2,1)}, u32[]{:S(2)}, u32[]{:S(2)}) collective-permute-start(bf16[128,2048]{1,0:T(8,128)(2,1)} %get-tuple-element.12), channel_id=1, source_target_pairs={{0,1},{1,0},{2,3},{3,2},{4,5},{5,4},{6,7},{7,6},{8,9},{9,8},{10,11... | collective-permute-start | bytes 1572872 | tf_op jit(solution)/shard_map/ppermute | solution.py:20
  7.8 4.7 %collective-permute-start.1 = (bf16[128,2048]{1,0:T(8,128)(2,1)}, bf16[128,2048]{1,0:T(8,128)(2,1)}, u32[]{:S(2)}, u32[]{:S(2)}) collective-permute-start(bf16[128,2048]{1,0:T(8,128)(2,1)} %get-tuple-element.13), channel_id=1, source_target_pairs={{0,1},{1,0},{2,3},{3,2},{4,5},{5,4},{6,7},{7,6},{8,9},{9,8},{10,11... | collective-permute-start | bytes 1572872 | tf_op jit(solution)/shard_map/ppermute | solution.py:20
  14.8 1.5 copy.58
  16.6 2.3 %copy.53 = f32[1,1,128,2048]{2,3,1,0:T(8,128)} copy(bf16[1,1,128,2048]{3,2,1,0:T(8,128)(2,1)} %param.7) | data formatting | bytes 1572864 | tf_op jit(solution)/shard_map/convert_element_type | solution.py:99
  20.6 12.6 %collective-permute-done = bf16[128,2048]{1,0:T(8,128)(2,1)} collective-permute-done((bf16[128,2048]{1,0:T(8,128)(2,1)}, bf16[128,2048]{1,0:T(8,128)(2,1)}, u32[]{:S(2)}, u32[]{:S(2)}) %collective-permute-start) | collective-permute-done | bytes 524320 | tf_op jit(solution)/shard_map/ppermute | solution.py:20
  35.6 3.9 %fusion.49 = (f32[16,128]{1,0:T(8,128)S(1)}, f32[16,128,256]{2,1,0:T(8,128)}) fusion(pred[256]{0:T(512)(128)(4,1)S(1)} %broadcast_bitcast_fusion.1, f32[16,128]{1,0:T(8,128)S(1)} %bitcast.124, f32[128,16,128]{0,2,1:T(8,128)} %broadcast_multiply_fusion.2, f32[128,16,128]{0,2,1:T(8,128)S(1)} %broadcast_multiply_fusion.3, f32[16,128]{1,0:T(8,128)S(1)} %bitcast.119), kind=kOutput, calls=%fused_computation.119 | convolution fusion | flops 138412288 | bytes 4219136 | tf_op jit(solution)/shard_map/sub | solution.py:68
  39.5 2.8 %fusion.26 = f32[16,128,256]{2,1,0:T(8,128)S(1)} fusion(f32[128,16,128]{0,2,1:T(8,128)} %bitcast.110, f32[16,128]{1,0:T(8,128)S(1)} %bitcast.141, f32[16,128,256]{2,1,0:T(8,128)} %get-tuple-element.24, f32[16,128]{1,0:T(8,128)S(1)} %get-tuple-element.23), kind=kOutput, calls=%fused_computation.70 | convolution fusion | flops 135790592 | bytes 5259264 | tf_op jit(solution)/shard_map/hts,thd->shd/dot_general | solution.py:123
  42.7 2.2 multiply_reduce_fusion.1
  45.6 1.9 fusion.5
  47.6 1.9 multiply_reduce_fusion.3
  50.5 6.3 %collective-permute-start.2 = (bf16[128,16,128]{0,2,1:T(8,128)(2,1)}, bf16[128,16,128]{0,2,1:T(8,128)(2,1)}, u32[]{:S(2)}, u32[]{:S(2)}) collective-permute-start(bf16[128,16,128]{0,2,1:T(8,128)(2,1)} %multiply_convert_fusion.7), channel_id=1, source_target_pairs={{0,1},{1,0},{2,3},{3,2},{4,5},{5,4},{6,7},{7,6},{8,9},{9,8},{10,11... | collective-permute-start | bytes 1572872 | tf_op jit(solution)/shard_map/ppermute | solution.py:20
  56.9 1.2 copy.59
  58.2 22.9 %collective-permute-done.2 = bf16[128,16,128]{0,2,1:T(8,128)(2,1)} collective-permute-done((bf16[128,16,128]{0,2,1:T(8,128)(2,1)}, bf16[128,16,128]{0,2,1:T(8,128)(2,1)}, u32[]{:S(2)}, u32[]{:S(2)}) %collective-permute-start.2) | collective-permute-done | bytes 524320 | tf_op jit(solution)/shard_map/ppermute | solution.py:20
  81.1 3.6 %convert_add_fusion = f32[128,16,128]{0,2,1:T(8,128)} fusion(bf16[128,16,128]{0,2,1:T(8,128)(2,1)} %collective-permute-done.2, f32[128,16,128]{0,2,1:T(8,128)} %bitcast.111, f32[128,16]{0,1:T(8,128)S(1)} %broadcast_multiply_fusion.7, f32[128,16]{0,1:T(8,128)S(1)} %add_rsqrt_fusion.3, f32[256,16,128]{0,2,1:T(8,128)} %copy-done.2, ...), kind=kLoop, calls=%fused_computation.45 | loop fusion | flops 2359296 | bytes 5791744 | tf_op jit(solution)/shard_map/add | solution.py:144
  84.7 2.6 %copy.62 = f32[128,2048]{1,0:T(8,128)} copy(f32[128,2048]{0,1:T(8,128)} %bitcast.114) | data formatting | bytes 2097152 | tf_op jit(solution)/shard_map/reshape | solution.py:148
  87.3 11.7 %collective-permute-start.3 = (f32[128,2048]{1,0:T(8,128)}, f32[128,2048]{1,0:T(8,128)}, u32[]{:S(2)}, u32[]{:S(2)}) collective-permute-start(f32[128,2048]{1,0:T(8,128)} %copy.62), channel_id=1, source_target_pairs={{16,0},{32,16},{48,32},{64,48},{80,64},{96,80},{112,96},{128,112},... | collective-permute-start | bytes 3145736 | tf_op jit(solution)/shard_map/ppermute | solution.py:26
  100.1 4.8 %fusion.50 = (f32[16,128]{1,0:T(8,128)S(1)}, f32[16,128,256]{2,1,0:T(8,128)}) fusion(pred[256]{0:T(512)(128)(4,1)S(1)} %broadcast_bitcast_fusion, f32[16,128]{1,0:T(8,128)S(1)} %bitcast.126, f32[128,16,128]{0,2,1:T(8,128)} %broadcast_multiply_fusion, f32[128,16,128]{0,2,1:T(8,128)} %broadcast_multiply_fusion.1, f32[16,128]{1,0:T(8,128)S(1)} %bitcast.121), kind=kOutput, calls=%fused_computation.120 | convolution fusion | flops 138412288 | bytes 4219136 | tf_op jit(solution)/shard_map/sub | solution.py:68
  104.9 2.6 %fusion.12 = f32[16,128]{1,0:T(8,128)S(1)} fusion(f32[128,16,128]{0,2,1:T(8,128)S(1)} %bitcast.113, f32[16,128]{1,0:T(8,128)S(1)} %bitcast.133, f32[128,16,128]{0,2,1:T(8,128)S(1)} %copy-done.1, f32[128,16,128]{0,2,1:T(8,128)S(1)} %broadcast_multiply_fusion.3, f32[16,128,256]{2,1,0:T(8,128)} %get-tuple-element.24, f32[16,128]{1,0:T(8,128)S(1)} %get-tuple-element.23), kind=kOutput, calls=%fused_computation.37 | convolution fusion | flops 137361408 | bytes 5267456 | tf_op jit(solution)/shard_map/hts,shd->thd/dot_general | solution.py:71
  107.5 14.2 %collective-permute-done.3 = f32[128,2048]{1,0:T(8,128)} collective-permute-done((f32[128,2048]{1,0:T(8,128)}, f32[128,2048]{1,0:T(8,128)}, u32[]{:S(2)}, u32[]{:S(2)}) %collective-permute-start.3) | collective-permute-done | bytes 1048608 | tf_op jit(solution)/shard_map/ppermute | solution.py:26
  121.7 1.3 convert_select_fusion
  123.1 1.3 copy.63
  124.4 3.4 %multiply_reduce_fusion = (f32[16,128]{1,0:T(8,128)S(1)}, f32[16,128,256]{2,1,0:T(8,128)S(1)}) fusion(f32[16,128,256]{2,1,0:T(8,128)S(1)} %copy-done.6, f32[16,128]{1,0:T(8,128)S(1)} %get-tuple-element.28, f32[16,128]{1,0:T(8,128)S(1)} %bitcast.134, f32[128,16,128]{0,2,1:T(8,128)} %broadcast_multiply_fusion, f32[128,16,128]{0,2,1:T(8,128)} %broadcast_multiply_fusion.1, ...), kind=kOutput, calls=%fused_computation.17 | convolution fusion | flops 137885696 | bytes 7372800 | tf_op jit(solution)/shard_map/thd,shd->hts/dot_general | solution.py:73
  133.7 86.5 %psum.7 = f32[1,4,2048]{2,1,0:T(4,128)} all-reduce(f32[1,4,2048]{2,1,0:T(4,128)S(1)} %fusion.32), channel_id=1, replica_groups=mesh['segment'=32,'dp'=8,'seq'=2] {'dp','seq'}, use_global_device_ids=true, to_apply=%region_22.23 | all-reduce | flops 8192 | bytes 65536 | tf_op jit(solution)/shard_map/psum | solution.py:154
  (68 shorter events, 15.7 us)
Async XLA Ops:
  0.0 12.8 %copy-start.13 = (s32[1,2,1,2]{3,2,1,0:T(1,128)S(1)}, s32[1,2,1,2]{3,2,1,0:T(1,128)}, u32[]{:S(2)}) copy-start(s32[1,2,1,2]{3,2,1,0:T(1,128)} %param.11) | copy-start | bytes 52
  0.0 12.8 %copy-start.12 = (s32[1,2,1,2,2]{4,3,2,1,0:T(2,128)S(1)}, s32[1,2,1,2,2]{4,3,2,1,0:T(2,128)}, u32[]{:S(2)}) copy-start(s32[1,2,1,2,2]{4,3,2,1,0:T(2,128)} %param.10) | copy-start | bytes 100
  2.7 30.5 %collective-permute-start = (bf16[128,2048]{1,0:T(8,128)(2,1)}, bf16[128,2048]{1,0:T(8,128)(2,1)}, u32[]{:S(2)}, u32[]{:S(2)}) collective-permute-start(bf16[128,2048]{1,0:T(8,128)(2,1)} %get-tuple-element.12), channel_id=1, source_target_pairs={{0,1},{1,0},{2,3},{3,2},{4,5},{5,4},{6,7},{7,6},{8,9},{9,8},{10,11... | collective-permute-start | bytes 1572872 | tf_op jit(solution)/shard_map/ppermute | solution.py:20
  7.8 49.1 %collective-permute-start.1 = (bf16[128,2048]{1,0:T(8,128)(2,1)}, bf16[128,2048]{1,0:T(8,128)(2,1)}, u32[]{:S(2)}, u32[]{:S(2)}) collective-permute-start(bf16[128,2048]{1,0:T(8,128)(2,1)} %get-tuple-element.13), channel_id=1, source_target_pairs={{0,1},{1,0},{2,3},{3,2},{4,5},{5,4},{6,7},{7,6},{8,9},{9,8},{10,11... | collective-permute-start | bytes 1572872 | tf_op jit(solution)/shard_map/ppermute | solution.py:20
  14.0 0.8 copy-start.11
  39.5 2.9 %copy-start = (f32[128,16,128]{0,2,1:T(8,128)S(1)}, f32[128,16,128]{0,2,1:T(8,128)}, u32[]{:S(2)}) copy-start(f32[128,16,128]{0,2,1:T(8,128)} %broadcast_multiply_fusion.2) | copy-start | bytes 3145732
  39.5 2.9 %copy-start.3 = (f32[1,1,128,2048]{2,3,1,0:T(8,128)S(1)}, f32[1,1,128,2048]{2,3,1,0:T(8,128)}, u32[]{:S(2)}) copy-start(f32[1,1,128,2048]{2,3,1,0:T(8,128)} %copy.53) | copy-start | bytes 3145732
  39.5 3.2 %copy-start.5 = (f32[16,128,256]{2,1,0:T(8,128)S(1)}, f32[16,128,256]{2,1,0:T(8,128)}, u32[]{:S(2)}) copy-start(f32[16,128,256]{2,1,0:T(8,128)} %get-tuple-element.24) | copy-start | bytes 6291460
  47.6 1.9 copy-start.2
  50.5 30.6 %collective-permute-start.2 = (bf16[128,16,128]{0,2,1:T(8,128)(2,1)}, bf16[128,16,128]{0,2,1:T(8,128)(2,1)}, u32[]{:S(2)}, u32[]{:S(2)}) collective-permute-start(bf16[128,16,128]{0,2,1:T(8,128)(2,1)} %multiply_convert_fusion.7), channel_id=1, source_target_pairs={{0,1},{1,0},{2,3},{3,2},{4,5},{5,4},{6,7},{7,6},{8,9},{9,8},{10,11... | collective-permute-start | bytes 1572872 | tf_op jit(solution)/shard_map/ppermute | solution.py:20
  87.3 34.4 %collective-permute-start.3 = (f32[128,2048]{1,0:T(8,128)}, f32[128,2048]{1,0:T(8,128)}, u32[]{:S(2)}, u32[]{:S(2)}) collective-permute-start(f32[128,2048]{1,0:T(8,128)} %copy.62), channel_id=1, source_target_pairs={{16,0},{32,16},{48,32},{64,48},{80,64},{96,80},{112,96},{128,112},... | collective-permute-start | bytes 3145736 | tf_op jit(solution)/shard_map/ppermute | solution.py:26
  100.1 4.8 %copy-start.1 = (f32[128,16,128]{0,2,1:T(8,128)S(1)}, f32[128,16,128]{0,2,1:T(8,128)}, u32[]{:S(2)}) copy-start(f32[128,16,128]{0,2,1:T(8,128)} %broadcast_multiply_fusion.2) | copy-start | bytes 3145732
  100.1 4.8 %copy-start.4 = (f32[1,1,128,2048]{2,3,1,0:T(8,128)S(1)}, f32[1,1,128,2048]{2,3,1,0:T(8,128)}, u32[]{:S(2)}) copy-start(f32[1,1,128,2048]{2,3,1,0:T(8,128)} %copy.53) | copy-start | bytes 3145732
  104.9 16.8 %copy-start.10 = (bf16[1,1,128,2048]{3,2,1,0:T(8,128)(2,1)S(1)}, bf16[1,1,128,2048]{3,2,1,0:T(8,128)(2,1)}, u32[]{:S(2)}) copy-start(bf16[1,1,128,2048]{3,2,1,0:T(8,128)(2,1)} %param.8) | copy-start | bytes 1572868
  107.5 16.9 %copy-start.6 = (f32[16,128,256]{2,1,0:T(8,128)S(1)}, f32[16,128,256]{2,1,0:T(8,128)}, u32[]{:S(2)}) copy-start(f32[16,128,256]{2,1,0:T(8,128)} %get-tuple-element.29) | copy-start | bytes 6291460
  127.8 1.2 copy-start.7
  127.8 1.5 copy-start.8
  130.0 1.2 copy-start.9
where the time goes:
time: 221 us; the launch traced here: 220 us
  blocking collectives  86.5 us (39%)
  waiting for transfers between devices  49.7 us (22%)
  starting transfers between devices  27.7 us (13%)
  matrix products  27.2 us (12%)
  other arithmetic  14.5 us (7%)
  local copies, waits for them, and re-layouts  14.3 us (6%)
    psum x1, blocking collectives, shards(): summed = lax.psum(totals.reshape(4, channels), ('dp', 'seq'))  86.5 us
    ppermute x3, waiting for transfers between devices, partner(): return lax.ppermute(block, axis, route)  35.5 us
    ppermute x3, starting transfers between devices, partner(): return lax.ppermute(block, axis, route)  16 us
    ppermute x1, waiting for transfers between devices, from_behind(): return lax.ppermute(block, axis, route)  14.2 us
    ppermute x1, starting transfers between devices, from_behind(): return lax.ppermute(block, axis, route)  11.7 us
    sub x2, matrix products, attend(): exped = jnp.exp(scores - jnp.max(scores, axis=-1, keepdims=True))  8.66 us
    dot_general x2, matrix products, attend(): jnp.einsum('thd,shd->hts', grad_out, val_mat, preferred_element_type=jnp....  5.55 us
  transfers between devices with their start and end apart: 4, of which 3 were waited for; matrix products, arithmetic and copies ran while one was open for 16% of the time, Pallas kernels for 0%

commit v1 on v0

v1 whole, which is shorter than its diff:
```python
import functools
import math

import jax
import jax.numpy as jnp
from jax import lax
from jax.experimental import pallas as pl
from jax.experimental.pallas import tpu as pltpu
from jax.sharding import PartitionSpec as P

HEAD_DIM = 128
BLK = 128
epsilon = 1e-06
MESH = pl.DeviceIdType.MESH
SCALE = HEAD_DIM ** (-0.5)
LOG2E = math.log2(math.e)
MASKED = -1e30

NT = (((1,), (1,)), ((), ()))
NN = (((1,), (0,)), ((), ()))
TN = (((0,), (0,)), ((), ()))


def mm(a, b, dims):
    return lax.dot_general(a, b, dims, preferred_element_type=jnp.float32)


def head_math(x, arr, gains, bias, with_input):
    g_query, g_key, g_val, gate = gains
    rows = x.shape[0]
    half = rows // 2
    xf = x.astype(jnp.float32)
    inv = lax.rsqrt(jnp.sum(xf * xf, axis=-1, keepdims=True) * (1.0 / HEAD_DIM) + epsilon)
    norm = xf * inv
    norm_low = norm.astype(jnp.bfloat16)
    qk = g_query * g_key
    vg = gate * g_val
    query = (norm * (qk * (SCALE * LOG2E))).astype(jnp.bfloat16)
    val = (norm * vg).astype(jnp.bfloat16)
    scores = mm(norm_low, query, NT)
    grad_probs = mm(val, arr, NT)
    lane = lax.broadcasted_iota(jnp.int32, (1, rows), 1)
    first = lane < half
    row_bias = [jnp.where(first, bias[c][0], bias[c][1]) for c in range(2)]
    parts = [scores[:half], scores[half:]]
    tops = [jnp.max(p, axis=0, keepdims=True) + b for p, b in zip(parts, row_bias)]
    top = jnp.maximum(tops[0], tops[1])
    exped = jnp.concatenate([jnp.exp2(p + (b - top)) for p, b in zip(parts, row_bias)], axis=0)
    probs = exped * (1.0 / jnp.sum(exped, axis=0, keepdims=True))
    weighted = probs * grad_probs
    grad_scores = weighted - probs * jnp.sum(weighted, axis=0, keepdims=True)
    ds = grad_scores.astype(jnp.bfloat16)
    back_val = mm(probs.astype(jnp.bfloat16), arr, NN)
    back_key = mm(ds, norm_low, NN)
    key_sum = jnp.sum(norm * back_key, axis=0, keepdims=True) * SCALE
    val_sum = jnp.sum(norm * back_val, axis=0, keepdims=True)
    if not with_input:
        return key_sum, val_sum, None
    back_query = mm(ds, norm_low, TN)
    u = (qk * SCALE) * (back_key + back_query) + vg * back_val
    centred = u - norm * (jnp.sum(u * norm, axis=-1, keepdims=True) * (1.0 / HEAD_DIM))
    grad_input = arr.astype(jnp.float32) + inv * centred
    return key_sum, val_sum, grad_input.astype(jnp.bfloat16)


def sweep_kernel(
    segments, n_dp, heads,
    x_ref, p_ref, u_ref, sf_ref, tab_ref, cnt_ref, out_ref,
    x_own, p_own, x_far, p_far, arr, gin, sfv, gath,
    lsem, x_s, x_r, p_s, p_r, arr_s, arr_r, red_s, red_r,
):
    seg = lax.axis_index("segment")
    dp = lax.axis_index("dp")
    seq = lax.axis_index("seq")
    far = {"seq": 1 - seq}
    below = {"segment": jnp.maximum(seg - 1, 0)}
    above = {"segment": jnp.minimum(seg + 1, segments - 1)}
    mine = pl.multiple_of(seq * (heads * HEAD_DIM), heads * HEAD_DIM)
    is_top = seg == segments - 1

    def group(d, s):
        return {"dp": lax.rem(dp + d, n_dp), "seq": lax.rem(seq + s, 2)}

    others = [(d, s) for s in range(2) for d in range(n_dp) if d + s > 0]

    width = heads * HEAD_DIM
    local = [
        pltpu.make_async_copy(x_ref.at[0, 0, 0, :, pl.ds(mine, width)], x_own.at[0], lsem.at[0]),
        pltpu.make_async_copy(p_ref.at[0, 0, :, pl.ds(mine, width)], p_own, lsem.at[1]),
        pltpu.make_async_copy(sf_ref.at[0], sfv, lsem.at[2]),
        pltpu.make_async_copy(x_ref.at[0, 1, 0, :, pl.ds(mine, width)], x_own.at[1], lsem.at[3]),
    ]
    for c in local:
        c.start()

    barrier = pltpu.get_barrier_semaphore()
    for d, s in others:
        pl.semaphore_signal(barrier, inc=1, device_id=group(d, s), device_id_type=MESH)

    @pl.when(seg > 0)
    def _():
        pl.semaphore_signal(barrier, inc=1, device_id=below, device_id_type=MESH)

    @pl.when(seg < segments - 1)
    def _():
        pl.semaphore_signal(barrier, inc=1, device_id=above, device_id_type=MESH)

    inner = jnp.where(seg > 0, 1, 0) + jnp.where(seg < segments - 1, 1, 0)
    pl.semaphore_wait(barrier, len(others) + inner)

    def far_cols(h):
        return pl.ds(pl.multiple_of(((1 - seq) * heads + h) * HEAD_DIM, HEAD_DIM), HEAD_DIM)

    def send_x(w, h):
        return pltpu.make_async_remote_copy(
            src_ref=x_ref.at[0, w, 0, :, far_cols(h)], dst_ref=x_far.at[w, h],
            send_sem=x_s.at[w, h], recv_sem=x_r.at[w, h], device_id=far, device_id_type=MESH,
        )

    def send_p(h):
        return pltpu.make_async_remote_copy(
            src_ref=p_ref.at[0, 0, :, far_cols(h)], dst_ref=p_far.at[h],
            send_sem=p_s.at[h], recv_sem=p_r.at[h], device_id=far, device_id_type=MESH,
        )

    def send_u(h):
        return pltpu.make_async_remote_copy(
            src_ref=u_ref.at[0, 0, :, far_cols(h)], dst_ref=arr.at[h, pl.ds(BLK, BLK)],
            send_sem=arr_s.at[h], recv_sem=arr_r.at[h], device_id=far, device_id_type=MESH,
        )

    def own_u(h):
        cols = pl.ds(pl.multiple_of(mine + h * HEAD_DIM, HEAD_DIM), HEAD_DIM)
        return pltpu.make_async_copy(
            u_ref.at[0, 0, :, cols], arr.at[h, pl.ds(0, BLK)], lsem.at[4 + h]
        )

    def send_down(h):
        return pltpu.make_async_remote_copy(
            src_ref=gin.at[h], dst_ref=arr.at[h],
            send_sem=p_s.at[heads + h], recv_sem=p_r.at[heads + h],
            device_id=below, device_id_type=MESH,
        )

    for h in range(2):
        send_x(0, h).start()
        send_p(h).start()

    def bias_of(w):
        rows = []
        for c in range(2):
            key_block = lax.rem(c + seq, 2)
            row = []
            for r in range(2):
                a = lax.rem(r + seq, 2)
                hit = (tab_ref[0, w, 0, a, 0] == key_block) | (
                    (cnt_ref[0, w, 0, a] > 1) & (tab_ref[0, w, 0, a, 1] == key_block)
                )
                row.append(jnp.where(hit, 0.0, MASKED).astype(jnp.float32))
            rows.append(row)
        return rows

    def gains_of(h):
        cols = pl.ds(pl.multiple_of(mine + h * HEAD_DIM, HEAD_DIM), HEAD_DIM)
        return [sfv[i : i + 1, cols] for i in range(4)]

    def head_cols(h):
        return pl.ds(pl.multiple_of(h * HEAD_DIM, HEAD_DIM), HEAD_DIM)

    slot = seq * n_dp + dp
    bias0 = bias_of(0)
    bias1 = bias_of(1)
    for c in local[:3]:
        c.wait()

    def first_batch(h, carry):
        send_x(0, h).wait_send()
        send_p(h).wait_send()

        @pl.when(h + 2 < heads)
        def _():
            send_x(0, h + 2).start()
            send_p(h + 2).start()

        @pl.when(h + 2 >= heads)
        def _():
            first = (h + 2 - heads) * 2
            send_x(1, first).start()
            send_x(1, first + 1).start()

        @pl.when(is_top)
        def _():
            own_u(h).start()
            send_u(h).start()

        send_x(0, h).wait_recv()
        send_p(h).wait_recv()
        x = jnp.concatenate([x_own[0, :, head_cols(h)], x_far[0, h]], axis=0)
        pend = jnp.concatenate([p_own[:, head_cols(h)], p_far[h]], axis=0)
        key_sum, val_sum, grad_input = head_math(x, pend, gains_of(h), bias0, True)
        gin[h] = grad_input

        @pl.when(seg > 0)
        def _():
            send_down(h).start()

        gath[slot, pl.ds(h, 1)] = key_sum
        gath[slot, pl.ds(heads + h, 1)] = val_sum
        return carry

    lax.fori_loop(0, heads, first_batch, 0)
    local[3].wait()

    def second_batch(h, carry):
        send_x(1, h).wait_send()

        @pl.when(h + 4 < heads)
        def _():
            send_x(1, h + 4).start()

        send_x(1, h).wait_recv()

        @pl.when(is_top)
        def _():
            own_u(h).wait()
            send_u(h).wait()

        @pl.when(seg < segments - 1)
        def _():
            send_down(h).wait_recv()

        x = jnp.concatenate([x_own[1, :, head_cols(h)], x_far[1, h]], axis=0)
        key_sum, val_sum, _ = head_math(x, arr[h], gains_of(h), bias1, False)
        gath[slot, pl.ds(h, 1)] += key_sum
        gath[slot, pl.ds(heads + h, 1)] += val_sum
        return carry

    lax.fori_loop(0, heads, second_batch, 0)

    shares = []
    for d, s in others:
        c = pltpu.make_async_remote_copy(
            src_ref=gath.at[slot], dst_ref=gath.at[slot],
            send_sem=red_s.at[s * n_dp + d], recv_sem=red_r.at[s * n_dp + d],
            device_id=group(d, s), device_id_type=MESH,
        )
        c.start()
        shares.append(c)

    @pl.when(seg > 0)
    def _():
        def drain(h, carry):
            send_down(h).wait_send()
            return carry

        lax.fori_loop(0, heads, drain, 0)

    for c in shares:
        c.wait()
    for s in range(2):
        total = gath[s * n_dp]
        for d in range(1, n_dp):
            total = total + gath[s * n_dp + d]
        for h in range(heads):
            cols = slice((s * heads + h) * HEAD_DIM, (s * heads + h + 1) * HEAD_DIM)
            key_sum = total[h : h + 1]
            val_sum = total[heads + h : heads + h + 1]
            out_ref[0, 0:1, cols] = sfv[1:2, cols] * key_sum
            out_ref[0, 1:2, cols] = sfv[0:1, cols] * key_sum
            out_ref[0, 2:3, cols] = sfv[3:4, cols] * val_sum
            out_ref[0, 3:4, cols] = sfv[2:3, cols] * val_sum


def shards(segments, n_dp, x, pend, top, gains, table, count):
    rows, channels = x.shape[3], x.shape[4]
    heads = channels // HEAD_DIM // 2
    width = heads * HEAD_DIM
    any_space = pl.BlockSpec(memory_space=pltpu.HBM)
    smem = pl.BlockSpec(memory_space=pltpu.SMEM)
    dma = pltpu.SemaphoreType.DMA
    low = jnp.bfloat16
    return pl.pallas_call(
        functools.partial(sweep_kernel, segments, n_dp, heads),
        out_shape=jax.ShapeDtypeStruct((1, 4, channels), jnp.float32),
        in_specs=[any_space] * 4 + [smem] * 2,
        out_specs=pl.BlockSpec(memory_space=pltpu.VMEM),
        scratch_shapes=[
            pltpu.VMEM((2, rows, width), low),
            pltpu.VMEM((rows, width), low),
            pltpu.VMEM((2, heads, rows, HEAD_DIM), low),
            pltpu.VMEM((heads, rows, HEAD_DIM), low),
            pltpu.VMEM((heads, 2 * rows, HEAD_DIM), low),
            pltpu.VMEM((heads, 2 * rows, HEAD_DIM), low),
            pltpu.VMEM((4, channels), jnp.float32),
            pltpu.VMEM((2 * n_dp, 2 * heads, HEAD_DIM), jnp.float32),
            dma((4 + heads,)),
            dma((2, heads)),
            dma((2, heads)),
            dma((2 * heads,)),
            dma((2 * heads,)),
            dma((heads,)),
            dma((heads,)),
            dma((2 * n_dp,)),
            dma((2 * n_dp,)),
        ],
        compiler_params=pltpu.CompilerParams(
            collective_id=1, has_side_effects=True, vmem_limit_bytes=48 << 20
        ),
        name="sweep",
    )(x, pend, top, gains, table, count)


def solution(mesh):
    placed = (
        P("segment", None, "dp", "seq", None),
        P("segment", "dp", "seq", None),
        P(None, "dp", "seq", None),
        P("segment", None, None),
        P("segment", None, "dp", None, None),
        P("segment", None, "dp", None),
    )
    body = functools.partial(shards, mesh.shape["segment"], mesh.shape["dp"])
    return jax.shard_map(
        body, mesh=mesh, in_specs=placed, out_specs=P("segment", None, None), check_vma=False
    )
```

time: 221 us -> 78 us (0.35)
  the two profiles are of different devices: /device:TPU:24 before, /device:TPU:9 now
where the time goes in v1:
time: 78 us; the launch traced here: 77.7 us
  Pallas kernels  71.6 us (92%)
  local copies, waits for them, and re-layouts  6.04 us (8%)
    pallas_call x1, Pallas kernels, shards(): pl.pallas_call(functools.partial(sweep_kernel, segments, n_dp, heads), ou...  71.6 us
    unnamed x13, local copies, waits for them, and re-layouts  6.04 us

profile of v1, /device:TPU:9, one launch (start us, length us, event | category | flops | bytes accessed | tf_op | source)
XLA Modules:
  0.0 77.7 jit_solution(9162489140178462493)
XLA Ops:
  0.0 0.0 copy-start
  0.0 1.2 %copy-done = bf16[1,2,1,128,2048]{4,3,2,1,0:T(8,128)(2,1)S(1)} copy-done((bf16[1,2,1,128,2048]{4,3,2,1,0:T(8,128)(2,1)S(1)}, bf16[1,2,1,128,2048]{4,3,2,1,0:T(8,128)(2,1)}, u32[]{:S(2)}) %copy-start) | copy-done | bytes 1048600
  1.2 0.0 copy-start.1
  1.2 1.0 %copy-done.1 = bf16[1,1,128,2048]{3,2,1,0:T(8,128)(2,1)S(1)} copy-done((bf16[1,1,128,2048]{3,2,1,0:T(8,128)(2,1)S(1)}, bf16[1,1,128,2048]{3,2,1,0:T(8,128)(2,1)}, u32[]{:S(2)}) %copy-start.1) | copy-done | bytes 524312
  2.3 0.0 copy-start.2
  2.3 1.0 %copy-done.2 = bf16[1,1,128,2048]{3,2,1,0:T(8,128)(2,1)S(1)} copy-done((bf16[1,1,128,2048]{3,2,1,0:T(8,128)(2,1)S(1)}, bf16[1,1,128,2048]{3,2,1,0:T(8,128)(2,1)}, u32[]{:S(2)}) %copy-start.2) | copy-done | bytes 524312
  3.3 0.0 copy-start.3
  3.3 0.8 copy-done.3
  4.1 0.0 copy-start.4
  4.1 0.7 copy-done.4
  4.8 0.0 copy-start.5
  4.8 0.7 copy-done.5
  5.4 71.6 %sweep.1 = f32[1,4,2048]{2,1,0:T(4,128)S(1)} custom-call(bf16[1,2,1,128,2048]{4,3,2,1,0:T(8,128)(2,1)S(1)} %copy-done, bf16[1,1,128,2048]{3,2,1,0:T(8,128)(2,1)S(1)} %copy-done.1, bf16[1,1,128,2048]{3,2,1,0:T(8,128)(2,1)S(1)} %copy-done.2, f32[1,4,2048]{2,1,0:T(4,128)S(1)} %copy-done.3, s32[1,2,1,2,2]{4,3,2,1,0:T(2,128)S(1)} %copy-done.4, ...), custom_call_target="tpu_custom_call" | custom-call | tf_op jit(solution)/shard_map/sweep/pallas_call | solution.py:282
  77.1 0.6 copy.8
Async XLA Ops:
  0.0 1.2 %copy-start = (bf16[1,2,1,128,2048]{4,3,2,1,0:T(8,128)(2,1)S(1)}, bf16[1,2,1,128,2048]{4,3,2,1,0:T(8,128)(2,1)}, u32[]{:S(2)}) copy-start(bf16[1,2,1,128,2048]{4,3,2,1,0:T(8,128)(2,1)} %x_ref.1) | copy-start | bytes 3145732
  1.2 1.0 %copy-start.1 = (bf16[1,1,128,2048]{3,2,1,0:T(8,128)(2,1)S(1)}, bf16[1,1,128,2048]{3,2,1,0:T(8,128)(2,1)}, u32[]{:S(2)}) copy-start(bf16[1,1,128,2048]{3,2,1,0:T(8,128)(2,1)} %p_ref.1) | copy-start | bytes 1572868
  2.3 1.0 %copy-start.2 = (bf16[1,1,128,2048]{3,2,1,0:T(8,128)(2,1)S(1)}, bf16[1,1,128,2048]{3,2,1,0:T(8,128)(2,1)}, u32[]{:S(2)}) copy-start(bf16[1,1,128,2048]{3,2,1,0:T(8,128)(2,1)} %u_ref.1) | copy-start | bytes 1572868
  3.3 0.8 copy-start.3
  4.1 0.7 copy-start.4
  4.8 0.7 copy-start.5

commit v2 on v1

--- a/solution.py
+++ b/solution.py
@@ -15,6 +15,9 @@
 SCALE = HEAD_DIM ** (-0.5)
 LOG2E = math.log2(math.e)
 MASKED = -1e30
+RUN = 8
+HELPERS = 3
+LENDERS = 4
 
 NT = (((1,), (1,)), ((), ()))
 NN = (((1,), (0,)), ((), ()))
@@ -66,47 +69,85 @@
 def sweep_kernel(
     segments, n_dp, heads,
     x_ref, p_ref, u_ref, sf_ref, tab_ref, cnt_ref, out_ref,
-    x_own, p_own, x_far, p_far, arr, gin, sfv, gath,
-    lsem, x_s, x_r, p_s, p_r, arr_s, arr_r, red_s, red_r,
+    x_own, p_own, x_far, p_far, arr, gin, passing, sfv, gath,
+    lsem, x_s, x_r, p_s, p_r, down_s, down_r, u_s, pass_s, pass_r, red_s, red_r, ready,
 ):
     seg = lax.axis_index("segment")
     dp = lax.axis_index("dp")
     seq = lax.axis_index("seq")
+    z = lax.rem(seg, RUN)
+    run = seg // RUN
+    rank = seq * n_dp + dp
+    far_rank = (1 - seq) * n_dp + dp
     far = {"seq": 1 - seq}
-    below = {"segment": jnp.maximum(seg - 1, 0)}
-    above = {"segment": jnp.minimum(seg + 1, segments - 1)}
     mine = pl.multiple_of(seq * (heads * HEAD_DIM), heads * HEAD_DIM)
+
     is_top = seg == segments - 1
-
-    def group(d, s):
-        return {"dp": lax.rem(dp + d, n_dp), "seq": lax.rem(seq + s, 2)}
-
-    others = [(d, s) for s in range(2) for d in range(n_dp) if d + s > 0]
-
+    edge_src = (z == 0) & (run > 0)
+    edge_dst = (z == RUN - 1) & (seg < segments - 1)
+    helper = (z > 0) & (z <= HELPERS) & (run > 0)
+    plain_src = z > 0
+    plain_dst = z < RUN - 1
+    lender = (seg >= RUN - LENDERS) & (seg < RUN)
+    borne = 2 * HELPERS
+    lent = heads // LENDERS
+
+    def at(section):
+        return {"segment": section}
+
+    def peer(t):
+        return {"dp": lax.rem(t, n_dp), "seq": t // n_dp}
+
+    def signal(sem, device):
+        pl.semaphore_signal(sem, inc=1, device_id=device, device_id_type=MESH)
+
+    barrier = pltpu.get_barrier_semaphore()
+    signal(barrier, far)
     width = heads * HEAD_DIM
     local = [
-        pltpu.make_async_copy(x_ref.at[0, 0, 0, :, pl.ds(mine, width)], x_own.at[0], lsem.at[0]),
-        pltpu.make_async_copy(p_ref.at[0, 0, :, pl.ds(mine, width)], p_own, lsem.at[1]),
         pltpu.make_async_copy(sf_ref.at[0], sfv, lsem.at[2]),
-        pltpu.make_async_copy(x_ref.at[0, 1, 0, :, pl.ds(mine, width)], x_own.at[1], lsem.at[3]),
+        pltpu.make_async_copy(x_ref.at[0, 0, 0, :, pl.ds(mine, width)], x_own.at[0], lsem.at[3]),
+        pltpu.make_async_copy(p_ref.at[0, 0, :, pl.ds(mine, width)], p_own, lsem.at[4]),
+        pltpu.make_async_copy(x_ref.at[0, 1, 0, :, pl.ds(mine, width)], x_own.at[1], lsem.at[5]),
     ]
     for c in local:
         c.start()
 
-    barrier = pltpu.get_barrier_semaphore()
-    for d, s in others:
-        pl.semaphore_signal(barrier, inc=1, device_id=group(d, s), device_id_type=MESH)
-
-    @pl.when(seg > 0)
-    def _():
-        pl.semaphore_signal(barrier, inc=1, device_id=below, device_id_type=MESH)
-
-    @pl.when(seg < segments - 1)
-    def _():
-        pl.semaphore_signal(barrier, inc=1, device_id=above, device_id_type=MESH)
-
-    inner = jnp.where(seg > 0, 1, 0) + jnp.where(seg < segments - 1, 1, 0)
-    pl.semaphore_wait(barrier, len(others) + inner)
+    @pl.when(plain_dst)
+    def _():
+        signal(barrier, at(seg + 1))
+
+    @pl.when(edge_src)
+    def _():
+        signal(barrier, at(seg - 1))
+        for k in range(1, HELPERS + 1):
+            signal(barrier, at(seg + k))
+
+    @pl.when(helper)
+    def _():
+        signal(barrier, at(seg - z - 1))
+
+    @pl.when(lender)
+    def _():
+        signal(barrier, {"segment": segments - 1, "seq": 1 - seq})
+
+    def greet(t, carry):
+        @pl.when(t != far_rank)
+        def _():
+            signal(barrier, peer(t))
+
+        return carry
+
+    lax.fori_loop(rank + 1, 2 * n_dp, greet, 0)
+
+    def one(cond, amount=1):
+        return jnp.where(cond, amount, 0)
+
+    earlier = rank - seq
+    pl.semaphore_wait(
+        barrier,
+        1 + earlier + one(plain_src) + one(edge_dst, 1 + HELPERS) + one(helper) + one(is_top, LENDERS),
+    )
 
     def far_cols(h):
         return pl.ds(pl.multiple_of(((1 - seq) * heads + h) * HEAD_DIM, HEAD_DIM), HEAD_DIM)
@@ -126,25 +167,64 @@
     def send_u(h):
         return pltpu.make_async_remote_copy(
             src_ref=u_ref.at[0, 0, :, far_cols(h)], dst_ref=arr.at[h, pl.ds(BLK, BLK)],
-            send_sem=arr_s.at[h], recv_sem=arr_r.at[h], device_id=far, device_id_type=MESH,
+            send_sem=u_s.at[h], recv_sem=down_r.at[h],
+            device_id={"segment": segments - 1, "seq": 1 - seq}, device_id_type=MESH,
         )
 
     def own_u(h):
         cols = pl.ds(pl.multiple_of(mine + h * HEAD_DIM, HEAD_DIM), HEAD_DIM)
         return pltpu.make_async_copy(
-            u_ref.at[0, 0, :, cols], arr.at[h, pl.ds(0, BLK)], lsem.at[4 + h]
+            u_ref.at[0, 0, :, cols], arr.at[h, pl.ds(0, BLK)], lsem.at[6 + h]
         )
 
     def send_down(h):
         return pltpu.make_async_remote_copy(
             src_ref=gin.at[h], dst_ref=arr.at[h],
-            send_sem=p_s.at[heads + h], recv_sem=p_r.at[heads + h],
-            device_id=below, device_id_type=MESH,
+            send_sem=down_s.at[h], recv_sem=down_r.at[h],
+            device_id=at(lax.rem(seg + segments - 1, segments)), device_id_type=MESH,
+        )
+
+    def send_helper(h):
+        return pltpu.make_async_remote_copy(
+            src_ref=gin.at[h], dst_ref=passing.at[lax.rem(h, 2)],
+            send_sem=down_s.at[h], recv_sem=pass_r.at[lax.rem(h, 2)],
+            device_id=at(seg + 1 + h // 2), device_id_type=MESH,
+        )
+
+    def send_on(j):
+        h = 2 * (z - 1) + j
+        return pltpu.make_async_remote_copy(
+            src_ref=passing.at[j], dst_ref=arr.at[h],
+            send_sem=pass_s.at[j], recv_sem=down_r.at[h],
+            device_id=at(seg - z - 1), device_id_type=MESH,
         )
 
     for h in range(2):
         send_x(0, h).start()
         send_p(h).start()
+
+    @pl.when(edge_dst)
+    def _():
+        for k in range(HELPERS + 1):
+            signal(ready.at[0], at(seg + 1 + k))
+
+    @pl.when(helper)
+    def _():
+        signal(ready.at[1], at(seg - z))
+
+    @pl.when(is_top)
+    def _():
+        for k in range(LENDERS):
+            signal(ready.at[2], {"segment": RUN - 1 - k, "seq": 1 - seq})
+
+    def answer(t, carry):
+        @pl.when(t != far_rank)
+        def _():
+            signal(ready.at[3], peer(t))
+
+        return carry
+
+    lax.fori_loop(0, rank, answer, 0)
 
     def bias_of(w):
         rows = []
@@ -167,11 +247,23 @@
     def head_cols(h):
         return pl.ds(pl.multiple_of(h * HEAD_DIM, HEAD_DIM), HEAD_DIM)
 
-    slot = seq * n_dp + dp
+    for c in local[:3]:
+        c.wait()
     bias0 = bias_of(0)
     bias1 = bias_of(1)
-    for c in local[:3]:
-        c.wait()
+
+    @pl.when(edge_src)
+    def _():
+        pl.semaphore_wait(ready.at[0], 1)
+        pl.semaphore_wait(ready.at[1], HELPERS)
+
+    @pl.when(helper)
+    def _():
+        pl.semaphore_wait(ready.at[0], 1)
+
+    @pl.when(lender)
+    def _():
+        pl.semaphore_wait(ready.at[2], 1)
 
     def first_batch(h, carry):
         send_x(0, h).wait_send()
@@ -191,6 +283,9 @@
         @pl.when(is_top)
         def _():
             own_u(h).start()
+
+        @pl.when(lender & (h // lent == RUN - 1 - seg))
+        def _():
             send_u(h).start()
 
         send_x(0, h).wait_recv()
@@ -200,12 +295,21 @@
         key_sum, val_sum, grad_input = head_math(x, pend, gains_of(h), bias0, True)
         gin[h] = grad_input
 
-        @pl.when(seg > 0)
+        @pl.when(plain_src | (edge_src & (h >= borne)))
         def _():
             send_down(h).start()
 
-        gath[slot, pl.ds(h, 1)] = key_sum
-        gath[slot, pl.ds(heads + h, 1)] = val_sum
+        @pl.when(edge_src & (h < borne))
+        def _():
+            send_helper(h).start()
+
+        @pl.when(helper & (h // 2 == z))
+        def _():
+            send_helper(h).wait_recv()
+            send_on(lax.rem(h, 2)).start()
+
+        gath[rank, pl.ds(h, 1)] = key_sum
+        gath[rank, pl.ds(heads + h, 1)] = val_sum
         return carry
 
     lax.fori_loop(0, heads, first_batch, 0)
@@ -223,7 +327,7 @@
         @pl.when(is_top)
         def _():
             own_u(h).wait()
-            send_u(h).wait()
+            send_u(h).wait_recv()
 
         @pl.when(seg < segments - 1)
         def _():
@@ -231,29 +335,45 @@
 
         x = jnp.concatenate([x_own[1, :, head_cols(h)], x_far[1, h]], axis=0)
         key_sum, val_sum, _ = head_math(x, arr[h], gains_of(h), bias1, False)
-        gath[slot, pl.ds(h, 1)] += key_sum
-        gath[slot, pl.ds(heads + h, 1)] += val_sum
+        gath[rank, pl.ds(h, 1)] += key_sum
+        gath[rank, pl.ds(heads + h, 1)] += val_sum
         return carry
 
     lax.fori_loop(0, heads, second_batch, 0)
 
+    later = 2 * n_dp - 1 - rank - (1 - seq)
+
+    @pl.when(later > 0)
+    def _():
+        pl.semaphore_wait(ready.at[3], later)
+
     shares = []
-    for d, s in others:
+    for d in range(1, 2 * n_dp):
+        to = lax.rem(rank + d, 2 * n_dp)
         c = pltpu.make_async_remote_copy(
-            src_ref=gath.at[slot], dst_ref=gath.at[slot],
-            send_sem=red_s.at[s * n_dp + d], recv_sem=red_r.at[s * n_dp + d],
-            device_id=group(d, s), device_id_type=MESH,
+            src_ref=gath.at[rank], dst_ref=gath.at[rank],
+            send_sem=red_s.at[d], recv_sem=red_r.at[d], device_id=peer(to), device_id_type=MESH,
         )
         c.start()
         shares.append(c)
 
-    @pl.when(seg > 0)
-    def _():
-        def drain(h, carry):
+    def drain_down(h, carry):
+        @pl.when(plain_src | edge_src)
+        def _():
             send_down(h).wait_send()
-            return carry
-
-        lax.fori_loop(0, heads, drain, 0)
+
+        @pl.when(lender & (h // lent == RUN - 1 - seg))
+        def _():
+            send_u(h).wait_send()
+
+        return carry
+
+    lax.fori_loop(0, heads, drain_down, 0)
+
+    @pl.when(helper)
+    def _():
+        for j in range(2):
+            send_on(j).wait_send()
 
     for c in shares:
         c.wait()
@@ -275,14 +395,13 @@
     rows, channels = x.shape[3], x.shape[4]
     heads = channels // HEAD_DIM // 2
     width = heads * HEAD_DIM
-    any_space = pl.BlockSpec(memory_space=pltpu.HBM)
-    smem = pl.BlockSpec(memory_space=pltpu.SMEM)
+    in_place = pl.BlockSpec(memory_space=pltpu.HBM)
     dma = pltpu.SemaphoreType.DMA
     low = jnp.bfloat16
     return pl.pallas_call(
         functools.partial(sweep_kernel, segments, n_dp, heads),
         out_shape=jax.ShapeDtypeStruct((1, 4, channels), jnp.float32),
-        in_specs=[any_space] * 4 + [smem] * 2,
+        in_specs=[in_place] * 4 + [pl.BlockSpec(memory_space=pltpu.SMEM)] * 2,
         out_specs=pl.BlockSpec(memory_space=pltpu.VMEM),
         scratch_shapes=[
             pltpu.VMEM((2, rows, width), low),
@@ -291,20 +410,25 @@
             pltpu.VMEM((heads, rows, HEAD_DIM), low),
             pltpu.VMEM((heads, 2 * rows, HEAD_DIM), low),
             pltpu.VMEM((heads, 2 * rows, HEAD_DIM), low),
+            pltpu.VMEM((2, 2 * rows, HEAD_DIM), low),
             pltpu.VMEM((4, channels), jnp.float32),
             pltpu.VMEM((2 * n_dp, 2 * heads, HEAD_DIM), jnp.float32),
-            dma((4 + heads,)),
+            dma((6 + heads,)),
             dma((2, heads)),
             dma((2, heads)),
-            dma((2 * heads,)),
-            dma((2 * heads,)),
             dma((heads,)),
             dma((heads,)),
+            dma((heads,)),
+            dma((heads,)),
+            dma((heads,)),
+            dma((2,)),
+            dma((2,)),
             dma((2 * n_dp,)),
             dma((2 * n_dp,)),
+            pltpu.SemaphoreType.REGULAR((4,)),
         ],
         compiler_params=pltpu.CompilerParams(
-            collective_id=1, has_side_effects=True, vmem_limit_bytes=48 << 20
+            collective_id=1, has_side_effects=True, vmem_limit_bytes=60 << 20
         ),
         name="sweep",
     )(x, pend, top, gains, table, count)

time: 78 us -> 62.7 us (0.80)
  the two profiles are of different devices: /device:TPU:9 before, /device:TPU:1 now
where the time goes in v2:
time: 62.7 us; the launch traced here: 61.6 us
  Pallas kernels  60.3 us (96%)
  local copies, waits for them, and re-layouts  1.38 us (2%)
    pallas_call x1, Pallas kernels, shards(): pl.pallas_call(functools.partial(sweep_kernel, segments, n_dp, heads), ou...  60.3 us
    unnamed x1, local copies, waits for them, and re-layouts  1.38 us

profile of v2, /device:TPU:1, one launch (start us, length us, event | category | flops | bytes accessed | tf_op | source)
XLA Modules:
  0.0 61.6 jit_solution(3221661393743640750)
XLA Ops:
  0.0 60.3 %sweep.1 = f32[1,4,2048]{2,1,0:T(4,128)} custom-call(bf16[1,2,1,128,2048]{4,3,2,1,0:T(8,128)(2,1)} %x_ref.1, bf16[1,1,128,2048]{3,2,1,0:T(8,128)(2,1)} %p_ref.1, bf16[1,1,128,2048]{3,2,1,0:T(8,128)(2,1)} %u_ref.1, f32[1,4,2048]{2,1,0:T(4,128)} %sf_ref.1, s32[1,2,1,2,2]{4,3,2,1,0:T(2,128)} %tab_ref.1, s32[1,2,1,2]{3,2,1,0:T(1,128)} %cnt_ref.1), custom_call_target="tpu_custom_call" | custom-call | tf_op jit(solution)/shard_map/sweep/pallas_call | solution.py:401
  60.3 1.4 %copy.8 = f32[1,4,2048]{2,1,0:T(4,128)} copy(f32[1,4,2048]{2,1,0:T(4,128)} %sweep.1) | data formatting | bytes 65536

commit v3 on v2

--- a/solution.py
+++ b/solution.py
@@ -16,8 +16,8 @@
 LOG2E = math.log2(math.e)
 MASKED = -1e30
 RUN = 8
-HELPERS = 3
-LENDERS = 4
+HELPERS = 7
+LENDERS = 8
 
 NT = (((1,), (1,)), ((), ()))
 NN = (((1,), (0,)), ((), ()))
@@ -69,8 +69,8 @@
 def sweep_kernel(
     segments, n_dp, heads,
     x_ref, p_ref, u_ref, sf_ref, tab_ref, cnt_ref, out_ref,
-    x_own, p_own, x_far, p_far, arr, gin, passing, sfv, gath,
-    lsem, x_s, x_r, p_s, p_r, down_s, down_r, u_s, pass_s, pass_r, red_s, red_r, ready,
+    x_own, p_own, x_far, p_far, arr, gin, passing, sfv, part, coll, mid, gath, table, count,
+    lsem, x_s, x_r, p_s, p_r, down_s, down_r, u_s, pass_s, pass_r, one_s, one_r, two_s, two_r, red_s, red_r, ready,
 ):
     seg = lax.axis_index("segment")
     dp = lax.axis_index("dp")
@@ -89,7 +89,8 @@
     plain_src = z > 0
     plain_dst = z < RUN - 1
     lender = (seg >= RUN - LENDERS) & (seg < RUN)
-    borne = 2 * HELPERS
+    borne = HELPERS
+    early = heads // 2
     lent = heads // LENDERS
 
     def at(section):
@@ -105,6 +106,8 @@
     signal(barrier, far)
     width = heads * HEAD_DIM
     local = [
+        pltpu.make_async_copy(tab_ref.at[0, :, 0], table, lsem.at[0]),
+        pltpu.make_async_copy(cnt_ref.at[0, :, 0], count, lsem.at[1]),
         pltpu.make_async_copy(sf_ref.at[0], sfv, lsem.at[2]),
         pltpu.make_async_copy(x_ref.at[0, 0, 0, :, pl.ds(mine, width)], x_own.at[0], lsem.at[3]),
         pltpu.make_async_copy(p_ref.at[0, 0, :, pl.ds(mine, width)], p_own, lsem.at[4]),
@@ -186,16 +189,15 @@
 
     def send_helper(h):
         return pltpu.make_async_remote_copy(
-            src_ref=gin.at[h], dst_ref=passing.at[lax.rem(h, 2)],
-            send_sem=down_s.at[h], recv_sem=pass_r.at[lax.rem(h, 2)],
-            device_id=at(seg + 1 + h // 2), device_id_type=MESH,
-        )
-
-    def send_on(j):
-        h = 2 * (z - 1) + j
-        return pltpu.make_async_remote_copy(
-            src_ref=passing.at[j], dst_ref=arr.at[h],
-            send_sem=pass_s.at[j], recv_sem=down_r.at[h],
+            src_ref=gin.at[h], dst_ref=passing,
+            send_sem=down_s.at[h], recv_sem=pass_r.at[0],
+            device_id=at(lax.rem(seg + 1 + h, segments)), device_id_type=MESH,
+        )
+
+    def send_on():
+        return pltpu.make_async_remote_copy(
+            src_ref=passing, dst_ref=arr.at[z - 1],
+            send_sem=pass_s.at[0], recv_sem=down_r.at[z - 1],
             device_id=at(seg - z - 1), device_id_type=MESH,
         )
 
@@ -210,17 +212,17 @@
 
     @pl.when(helper)
     def _():
-        signal(ready.at[1], at(seg - z))
+        signal(ready.at[2 + z], at(seg - z))
 
     @pl.when(is_top)
     def _():
         for k in range(LENDERS):
-            signal(ready.at[2], {"segment": RUN - 1 - k, "seq": 1 - seq})
+            signal(ready.at[1], {"segment": RUN - 1 - k, "seq": 1 - seq})
 
     def answer(t, carry):
         @pl.when(t != far_rank)
         def _():
-            signal(ready.at[3], peer(t))
+            signal(ready.at[2], peer(t))
 
         return carry
 
@@ -233,8 +235,8 @@
             row = []
             for r in range(2):
                 a = lax.rem(r + seq, 2)
-                hit = (tab_ref[0, w, 0, a, 0] == key_block) | (
-                    (cnt_ref[0, w, 0, a] > 1) & (tab_ref[0, w, 0, a, 1] == key_block)
+                hit = (table[w, a, 0] == key_block) | (
+                    (count[w, a] > 1) & (table[w, a, 1] == key_block)
                 )
                 row.append(jnp.where(hit, 0.0, MASKED).astype(jnp.float32))
             rows.append(row)
@@ -247,24 +249,11 @@
     def head_cols(h):
         return pl.ds(pl.multiple_of(h * HEAD_DIM, HEAD_DIM), HEAD_DIM)
 
-    for c in local[:3]:
+    for c in local[:5]:
         c.wait()
     bias0 = bias_of(0)
     bias1 = bias_of(1)
 
-    @pl.when(edge_src)
-    def _():
-        pl.semaphore_wait(ready.at[0], 1)
-        pl.semaphore_wait(ready.at[1], HELPERS)
-
-    @pl.when(helper)
-    def _():
-        pl.semaphore_wait(ready.at[0], 1)
-
-    @pl.when(lender)
-    def _():
-        pl.semaphore_wait(ready.at[2], 1)
-
     def first_batch(h, carry):
         send_x(0, h).wait_send()
         send_p(h).wait_send()
@@ -286,6 +275,7 @@
 
         @pl.when(lender & (h // lent == RUN - 1 - seg))
         def _():
+            pl.semaphore_wait(ready.at[1], 1)
             send_u(h).start()
 
         send_x(0, h).wait_recv()
@@ -295,25 +285,55 @@
         key_sum, val_sum, grad_input = head_math(x, pend, gains_of(h), bias0, True)
         gin[h] = grad_input
 
+        @pl.when(edge_src & (h == borne))
+        def _():
+            pl.semaphore_wait(ready.at[0], 1)
+
         @pl.when(plain_src | (edge_src & (h >= borne)))
         def _():
             send_down(h).start()
 
         @pl.when(edge_src & (h < borne))
         def _():
+            pl.semaphore_wait(ready.at[3 + h], 1)
             send_helper(h).start()
 
-        @pl.when(helper & (h // 2 == z))
-        def _():
-            send_helper(h).wait_recv()
-            send_on(lax.rem(h, 2)).start()
-
-        gath[rank, pl.ds(h, 1)] = key_sum
-        gath[rank, pl.ds(heads + h, 1)] = val_sum
+        @pl.when(helper & (h == z))
+        def _():
+            pl.semaphore_wait(ready.at[0], 1)
+            send_helper(h - 1).wait_recv()
+            send_on().start()
+
+        @pl.when(h < early)
+        def _():
+            part[h] = key_sum
+            part[early + h] = val_sum
+
+        @pl.when(h >= early)
+        def _():
+            gath[rank, pl.ds(h - early, 1)] = key_sum
+            gath[rank, pl.ds(h, 1)] = val_sum
+
         return carry
 
     lax.fori_loop(0, heads, first_batch, 0)
-    local[3].wait()
+    local[5].wait()
+
+    later = 2 * n_dp - 1 - rank - (1 - seq)
+
+    def send_part(d):
+        to = lax.rem(dp + d, n_dp)
+        return pltpu.make_async_remote_copy(
+            src_ref=part.at[to], dst_ref=coll.at[dp],
+            send_sem=one_s.at[d], recv_sem=one_r.at[d], device_id={"dp": to}, device_id_type=MESH,
+        )
+
+    def send_mid(d):
+        return pltpu.make_async_remote_copy(
+            src_ref=mid.at[rank], dst_ref=mid.at[rank],
+            send_sem=two_s.at[d], recv_sem=two_r.at[d],
+            device_id=peer(lax.rem(rank + d, 2 * n_dp)), device_id_type=MESH,
+        )
 
     def second_batch(h, carry):
         send_x(1, h).wait_send()
@@ -335,17 +355,40 @@
 
         x = jnp.concatenate([x_own[1, :, head_cols(h)], x_far[1, h]], axis=0)
         key_sum, val_sum, _ = head_math(x, arr[h], gains_of(h), bias1, False)
-        gath[rank, pl.ds(h, 1)] += key_sum
-        gath[rank, pl.ds(heads + h, 1)] += val_sum
+        @pl.when(h < early)
+        def _():
+            part[h] += key_sum
+            part[early + h] += val_sum
+
+        @pl.when(h >= early)
+        def _():
+            gath[rank, pl.ds(h - early, 1)] += key_sum
+            gath[rank, pl.ds(h, 1)] += val_sum
+
+        @pl.when(h == early - 1)
+        def _():
+            @pl.when(later > 0)
+            def _():
+                pl.semaphore_wait(ready.at[2], later)
+
+            coll[dp] = part[dp]
+            for d in range(1, n_dp):
+                send_part(d).start()
+
+        @pl.when(h == heads - 2)
+        def _():
+            for d in range(1, n_dp):
+                send_part(d).wait_recv()
+            total = coll[0]
+            for d in range(1, n_dp):
+                total = total + coll[d]
+            mid[rank] = total
+            for d in range(1, 2 * n_dp):
+                send_mid(d).start()
+
         return carry
 
     lax.fori_loop(0, heads, second_batch, 0)
-
-    later = 2 * n_dp - 1 - rank - (1 - seq)
-
-    @pl.when(later > 0)
-    def _():
-        pl.semaphore_wait(ready.at[3], later)
 
     shares = []
     for d in range(1, 2 * n_dp):
@@ -357,38 +400,50 @@
         c.start()
         shares.append(c)
 
-    def drain_down(h, carry):
-        @pl.when(plain_src | edge_src)
-        def _():
-            send_down(h).wait_send()
-
-        @pl.when(lender & (h // lent == RUN - 1 - seg))
-        def _():
-            send_u(h).wait_send()
-
-        return carry
-
-    lax.fori_loop(0, heads, drain_down, 0)
-
-    @pl.when(helper)
-    def _():
-        for j in range(2):
-            send_on(j).wait_send()
-
+    for d in range(1, 2 * n_dp):
+        send_mid(d).wait_recv()
     for c in shares:
-        c.wait()
+        c.wait_recv()
     for s in range(2):
         total = gath[s * n_dp]
         for d in range(1, n_dp):
             total = total + gath[s * n_dp + d]
         for h in range(heads):
             cols = slice((s * heads + h) * HEAD_DIM, (s * heads + h + 1) * HEAD_DIM)
-            key_sum = total[h : h + 1]
-            val_sum = total[heads + h : heads + h + 1]
+            if h < early:
+                key_sum = mid[s * n_dp + h]
+                val_sum = mid[s * n_dp + early + h]
+            else:
+                key_sum = total[h - early : h - early + 1]
+                val_sum = total[h : h + 1]
             out_ref[0, 0:1, cols] = sfv[1:2, cols] * key_sum
             out_ref[0, 1:2, cols] = sfv[0:1, cols] * key_sum
             out_ref[0, 2:3, cols] = sfv[3:4, cols] * val_sum
             out_ref[0, 3:4, cols] = sfv[2:3, cols] * val_sum
+
+    def drain_down(h, carry):
+        @pl.when(plain_src | edge_src)
+        def _():
+            send_down(h).wait_send()
+
+        @pl.when(lender & (h // lent == RUN - 1 - seg))
+        def _():
+            send_u(h).wait_send()
+
+        return carry
+
+    lax.fori_loop(0, heads, drain_down, 0)
+
+    @pl.when(helper)
+    def _():
+        send_on().wait_send()
+
+    for d in range(1, n_dp):
+        send_part(d).wait_send()
+    for d in range(1, 2 * n_dp):
+        send_mid(d).wait_send()
+    for c in shares:
+        c.wait_send()
 
 
 def shards(segments, n_dp, x, pend, top, gains, table, count):
@@ -401,7 +456,7 @@
     return pl.pallas_call(
         functools.partial(sweep_kernel, segments, n_dp, heads),
         out_shape=jax.ShapeDtypeStruct((1, 4, channels), jnp.float32),
-        in_specs=[in_place] * 4 + [pl.BlockSpec(memory_space=pltpu.SMEM)] * 2,
+        in_specs=[in_place] * 6,
         out_specs=pl.BlockSpec(memory_space=pltpu.VMEM),
         scratch_shapes=[
             pltpu.VMEM((2, rows, width), low),
@@ -410,9 +465,14 @@
             pltpu.VMEM((heads, rows, HEAD_DIM), low),
             pltpu.VMEM((heads, 2 * rows, HEAD_DIM), low),
             pltpu.VMEM((heads, 2 * rows, HEAD_DIM), low),
-            pltpu.VMEM((2, 2 * rows, HEAD_DIM), low),
+            pltpu.VMEM((2 * rows, HEAD_DIM), low),
             pltpu.VMEM((4, channels), jnp.float32),
-            pltpu.VMEM((2 * n_dp, 2 * heads, HEAD_DIM), jnp.float32),
+            pltpu.VMEM((n_dp, 1, HEAD_DIM), jnp.float32),
+            pltpu.VMEM((n_dp, 1, HEAD_DIM), jnp.float32),
+            pltpu.VMEM((2 * n_dp, 1, HEAD_DIM), jnp.float32),
+            pltpu.VMEM((2 * n_dp, heads, HEAD_DIM), jnp.float32),
+            pltpu.SMEM((2, 2, 2), jnp.int32),
+            pltpu.SMEM((2, 2), jnp.int32),
             dma((6 + heads,)),
             dma((2, heads)),
             dma((2, heads)),
@@ -421,17 +481,21 @@
             dma((heads,)),
             dma((heads,)),
             dma((heads,)),
-            dma((2,)),
-            dma((2,)),
+            dma((1,)),
+            dma((1,)),
+            dma((n_dp,)),
+            dma((n_dp,)),
             dma((2 * n_dp,)),
             dma((2 * n_dp,)),
-            pltpu.SemaphoreType.REGULAR((4,)),
+            dma((2 * n_dp,)),
+            dma((2 * n_dp,)),
+            pltpu.SemaphoreType.REGULAR((3 + HELPERS,)),
         ],
         compiler_params=pltpu.CompilerParams(
-            collective_id=1, has_side_effects=True, vmem_limit_bytes=60 << 20
+            collective_id=1, has_side_effects=True, vmem_limit_bytes=32 << 20
         ),
         name="sweep",
-    )(x, pend, top, gains, table, count)
+    )(*[pltpu.with_memory_space_constraint(v, pltpu.HBM) for v in (x, pend, top, gains, table, count)])
 
 
 def solution(mesh):

time: 62.7 us -> 59.8 us (0.954); the launches traced: 61.6 us -> 59.7 us
  Pallas kernels: 60.3 us -> 59 us
  local copies, waits for them, and re-layouts: 1.38 us -> 0.62 us
    pallas_call x1, Pallas kernels: 60.3 us -> 59 us  [shards(): pl.pallas_call(functools.partial(sweep_kernel, segments, n_dp, heads), ou...]
    unnamed x1, local copies, waits for them, and re-layouts: 1.38 us -> 0.62 us
where the time goes in v3:
time: 59.8 us; the launch traced here: 59.7 us
  Pallas kernels  59 us (99%)
  local copies, waits for them, and re-layouts  0.62 us (1%)
    pallas_call x1, Pallas kernels, shards(): pl.pallas_call(functools.partial(sweep_kernel, segments, n_dp, heads), ou...  59 us

profile of v3, /device:TPU:1, one launch (start us, length us, event | category | flops | bytes accessed | tf_op | source)
XLA Modules:
  0.0 59.7 jit_solution(9081230255530613918)
XLA Ops:
  0.0 59.0 %sweep.1 = f32[1,4,2048]{2,1,0:T(4,128)S(1)} custom-call(bf16[1,2,1,128,2048]{4,3,2,1,0:T(8,128)(2,1)} %x_ref.1, bf16[1,1,128,2048]{3,2,1,0:T(8,128)(2,1)} %p_ref.1, bf16[1,1,128,2048]{3,2,1,0:T(8,128)(2,1)} %u_ref.1, f32[1,4,2048]{2,1,0:T(4,128)} %sf_ref.1, s32[1,2,1,2,2]{4,3,2,1,0:T(2,128)} %tab_ref.1, s32[1,2,1,2]{3,2,1,0:T(1,128)} %cnt_ref.1), custom_call_target="tpu_custom_call" | custom-call | tf_op jit(solution)/shard_map/sweep/pallas_call | solution.py:456
  59.1 0.6 %copy.8 = f32[1,4,2048]{2,1,0:T(4,128)} copy(f32[1,4,2048]{2,1,0:T(4,128)S(1)} %sweep.1) | data formatting | bytes 65536

commit v4 on v3

v4 whole, which is shorter than its diff:
```python
import functools
import math

import jax
import jax.numpy as jnp
from jax import lax
from jax.experimental import pallas as pl
from jax.experimental.pallas import tpu as pltpu
from jax.sharding import PartitionSpec as P

HEAD_DIM = 128
BLK = 128
epsilon = 1e-06
MESH = pl.DeviceIdType.MESH
SCALE = HEAD_DIM ** (-0.5)
LOG2E = math.log2(math.e)
MASKED = -1e30
RUN = 8
LOOK = 4
HELPERS = 7
LENDERS = 8

NT = (((1,), (1,)), ((), ()))
NN = (((1,), (0,)), ((), ()))
TN = (((0,), (0,)), ((), ()))


def mm(a, b, dims):
    return lax.dot_general(a, b, dims, preferred_element_type=jnp.float32)


def head_math(x, arr, qk, vg, row_bias, with_input):
    rows = x.shape[0]
    half = rows // 2
    xf = x.astype(jnp.float32)
    inv = lax.rsqrt(jnp.sum(xf * xf, axis=-1, keepdims=True) * (1.0 / HEAD_DIM) + epsilon)
    norm = xf * inv
    norm_low = norm.astype(jnp.bfloat16)
    query = (norm * (qk * (SCALE * LOG2E))).astype(jnp.bfloat16)
    val = (norm * vg).astype(jnp.bfloat16)
    scores = mm(norm_low, query, NT)
    grad_probs = mm(val, arr, NT)
    parts = [scores[:half], scores[half:]]
    tops = [jnp.max(p, axis=0, keepdims=True) + b for p, b in zip(parts, row_bias)]
    top = jnp.maximum(tops[0], tops[1])
    exped = jnp.concatenate([jnp.exp2(p + (b - top)) for p, b in zip(parts, row_bias)], axis=0)
    probs = exped * (1.0 / jnp.sum(exped, axis=0, keepdims=True))
    weighted = probs * grad_probs
    grad_scores = weighted - probs * jnp.sum(weighted, axis=0, keepdims=True)
    ds = grad_scores.astype(jnp.bfloat16)
    back_val = mm(probs.astype(jnp.bfloat16), arr, NN)
    back_key = mm(ds, norm_low, NN)
    key_sum = jnp.sum(norm * back_key, axis=0, keepdims=True) * SCALE
    val_sum = jnp.sum(norm * back_val, axis=0, keepdims=True)
    if not with_input:
        return key_sum, val_sum, None
    back_query = mm(ds, norm_low, TN)
    u = (qk * SCALE) * (back_key + back_query) + vg * back_val
    centred = u - norm * (jnp.sum(u * norm, axis=-1, keepdims=True) * (1.0 / HEAD_DIM))
    grad_input = arr.astype(jnp.float32) + inv * centred
    return key_sum, val_sum, grad_input.astype(jnp.bfloat16)


def sweep_kernel(
    segments, n_dp, heads,
    x_ref, p_ref, u_ref, sf_ref, tab_ref, cnt_ref, out_ref,
    x_in, p_in, arr, gin, passing, sfv, meta, meta_in, part, late, coll, tot, mid, gath, table, count,
    lsem, x_s, x_r, p_s, p_r, m_s, m_r, down_s, down_r, u_s, pass_s, pass_r,
    one_s, one_r, two_s, two_r, red_s, red_r, ready,
):
    seg = lax.axis_index("segment")
    dp = lax.axis_index("dp")
    seq = lax.axis_index("seq")
    z = lax.rem(seg, RUN)
    run = seg // RUN
    ring = 2 * (segments // RUN)
    y = seq * (ring // 2) + run
    reach = ring // 4

    def place(dy, zz=None, to_dp=None):
        yy = lax.rem(y + dy + 2 * ring, ring)
        where = {
            "segment": lax.rem(yy, ring // 2) * RUN + (z if zz is None else zz),
            "seq": yy // (ring // 2),
        }
        if to_dp is not None:
            where["dp"] = to_dp
        return where

    sides = (-reach, reach)
    work = lax.rem(seg + segments // 2, segments)
    work_run = work // RUN

    def heads_at(dy):
        return lax.rem(y + dy + reach + 2 * ring, ring) // (ring // 2)

    here = heads_at(0)
    seq_of_side = (1 - here, here)

    is_top = work == segments - 1
    edge_src = (z == 0) & (work_run > 0)
    edge_dst = (z == RUN - 1) & (work < segments - 1)
    helper = (z > 0) & (work_run > 0)
    plain_src = z > 0
    plain_dst = z < RUN - 1
    lender = run == segments // RUN - 1
    borne = HELPERS
    early = heads // 2

    def at(section):
        return {"segment": section}

    def signal(sem, device):
        pl.semaphore_signal(sem, inc=1, device_id=device, device_id_type=MESH)

    barrier = pltpu.get_barrier_semaphore()
    for dy in sides:
        signal(barrier, place(dy))
    local = [
        pltpu.make_async_copy(tab_ref.at[0, :, 0], table, lsem.at[0]),
        pltpu.make_async_copy(cnt_ref.at[0, :, 0], count, lsem.at[1]),
        pltpu.make_async_copy(sf_ref.at[0], sfv, lsem.at[2]),
    ]
    for c in local:
        c.start()

    @pl.when(plain_dst)
    def _():
        signal(barrier, at(seg + 1))

    @pl.when(edge_src)
    def _():
        signal(barrier, place(-1, RUN - 1))
        for k in range(1, HELPERS + 1):
            signal(barrier, at(lax.rem(seg + k, segments)))

    @pl.when(helper)
    def _():
        signal(barrier, place(-1, RUN - 1))

    top_at = {"segment": segments // 2 - 1, "seq": 1 - seq}

    @pl.when(lender)
    def _():
        signal(barrier, top_at)

    def greet(t, carry):
        signal(barrier, place(0, None, t))
        return carry

    lax.fori_loop(dp + 1, n_dp, greet, 0)
    higher = [lax.rem(y + dy + ring, ring) > y for dy in sides]
    for dy, up in zip(sides, higher):
        @pl.when(up)
        def _():
            for d in range(1, n_dp):
                signal(barrier, place(dy, None, lax.rem(dp + d, n_dp)))

    def one(cond, amount=1):
        return jnp.where(cond, amount, 0)

    pl.semaphore_wait(
        barrier,
        2 + dp + sum(one(~up, n_dp - 1) for up in higher) + one(plain_src)
        + one(edge_dst, 1 + HELPERS) + one(helper) + one(is_top, LENDERS),
    )

    def cols_of(group, h):
        return pl.ds(pl.multiple_of((group * heads + h) * HEAD_DIM, HEAD_DIM), HEAD_DIM)

    def send_x(w, k, h):
        dy = (reach, -reach)[k]
        return pltpu.make_async_remote_copy(
            src_ref=x_ref.at[0, w, 0, :, cols_of(heads_at(dy), h)], dst_ref=x_in.at[w, k, h],
            send_sem=x_s.at[w, k, h], recv_sem=x_r.at[w, k, h],
            device_id=place(dy), device_id_type=MESH,
        )

    def send_p(k, h):
        dy = (reach, -reach)[k]
        return pltpu.make_async_remote_copy(
            src_ref=p_ref.at[0, 0, :, cols_of(heads_at(dy), h)], dst_ref=p_in.at[k, h],
            send_sem=p_s.at[k, h], recv_sem=p_r.at[k, h],
            device_id=place(dy), device_id_type=MESH,
        )

    def send_meta():
        return pltpu.make_async_remote_copy(
            src_ref=meta, dst_ref=meta_in, send_sem=m_s.at[0], recv_sem=m_r.at[0],
            device_id=place(reach), device_id_type=MESH,
        )

    def send_u(h):
        return pltpu.make_async_remote_copy(
            src_ref=u_ref.at[0, 0, :, cols_of(1 - seq, h)], dst_ref=arr.at[h, pl.ds(0, BLK)],
            send_sem=u_s.at[h], recv_sem=down_r.at[h], device_id=top_at, device_id_type=MESH,
        )

    def own_u(h):
        return pltpu.make_async_copy(
            u_ref.at[0, 0, :, cols_of(here, h)], arr.at[h, pl.ds(BLK, BLK)], lsem.at[3 + h]
        )

    def send_down(h):
        return pltpu.make_async_remote_copy(
            src_ref=gin.at[h], dst_ref=arr.at[h],
            send_sem=down_s.at[h], recv_sem=down_r.at[h],
            device_id=at(lax.rem(seg + segments - 1, segments)), device_id_type=MESH,
        )

    def send_edge(h):
        return pltpu.make_async_remote_copy(
            src_ref=gin.at[h], dst_ref=arr.at[h],
            send_sem=down_s.at[h], recv_sem=down_r.at[h],
            device_id=place(-1, RUN - 1), device_id_type=MESH,
        )

    def send_helper(h):
        return pltpu.make_async_remote_copy(
            src_ref=gin.at[h], dst_ref=passing,
            send_sem=down_s.at[h], recv_sem=pass_r.at[0],
            device_id=at(lax.rem(seg + 1 + h, segments)), device_id_type=MESH,
        )

    def send_on():
        return pltpu.make_async_remote_copy(
            src_ref=passing, dst_ref=arr.at[z - 1],
            send_sem=pass_s.at[0], recv_sem=down_r.at[z - 1],
            device_id=place(-1, RUN - 1), device_id_type=MESH,
        )

    for h in range(LOOK):
        for k in range(2):
            send_x(0, k, h).start()
            send_p(k, h).start()

    for c in local:
        c.wait()
    ahead = heads_at(reach)
    for h in range(heads):
        cols = cols_of(ahead, h)
        meta[h : h + 1] = sfv[0:1, cols] * sfv[1:2, cols]
        meta[heads + h : heads + h + 1] = sfv[3:4, cols] * sfv[2:3, cols]
    for w in range(2):
        for c in range(2):
            for a in range(2):
                hit = (table[w, a, 0] == c) | ((count[w, a] > 1) & (table[w, a, 1] == c))
                row = 2 * heads + 4 * w + 2 * c + a
                value = jnp.where(hit, 0.0, MASKED).astype(jnp.float32)
                meta[row : row + 1] = jnp.full((1, HEAD_DIM), value, jnp.float32)
    send_meta().start()

    @pl.when(edge_dst)
    def _():
        for k in range(HELPERS + 1):
            signal(ready.at[0], place(1, k))

    @pl.when(helper)
    def _():
        signal(ready.at[2 + z], at(seg - z))

    @pl.when(is_top)
    def _():
        for k in range(LENDERS):
            signal(ready.at[1], {"segment": segments - RUN + k, "seq": 1 - seq})

    def answer(t, carry):
        signal(ready.at[2], place(0, None, t))
        return carry

    lax.fori_loop(0, dp, answer, 0)
    for dy, up in zip(sides, higher):
        @pl.when(~up)
        def _():
            for d in range(1, n_dp):
                signal(ready.at[2], place(dy, None, lax.rem(dp + d, n_dp)))

    later = n_dp - 1 - dp + sum(one(up, n_dp - 1) for up in higher)

    def bias_of(w):
        rows = []
        for c in range(2):
            base = 2 * heads + 4 * w + 2 * seq_of_side[c]
            rows.append(
                jnp.concatenate(
                    [meta_in[pl.ds(base + seq_of_side[r], 1)] for r in range(2)], axis=1
                )
            )
        return rows

    def first_batch(h, carry):
        for k in range(2):
            send_x(0, k, h).wait_send()
            send_p(k, h).wait_send()

            @pl.when(h + LOOK < heads)
            def _():
                send_x(0, k, h + LOOK).start()
                send_p(k, h + LOOK).start()

            @pl.when(h + LOOK >= heads)
            def _():
                first = (h + LOOK - heads) * 2
                send_x(1, k, first).start()
                send_x(1, k, first + 1).start()

        @pl.when(is_top)
        def _():
            own_u(h).start()

        @pl.when(lender & (h == heads - 1 - z))
        def _():
            pl.semaphore_wait(ready.at[1], 1)
            send_u(h).start()

        @pl.when(h == 0)
        def _():
            send_meta().wait_recv()

        for k in range(2):
            send_x(0, k, h).wait_recv()
            send_p(k, h).wait_recv()
        x = jnp.concatenate([x_in[0, 0, h], x_in[0, 1, h]], axis=0)
        pend = jnp.concatenate([p_in[0, h], p_in[1, h]], axis=0)
        key_sum, val_sum, grad_input = head_math(
            x, pend, meta_in[pl.ds(h, 1)], meta_in[pl.ds(heads + h, 1)], bias_of(0), True
        )
        gin[h] = grad_input

        @pl.when(plain_src)
        def _():
            send_down(h).start()

        @pl.when(edge_src & (h < borne))
        def _():
            pl.semaphore_wait(ready.at[3 + h], 1)
            send_helper(h).start()

        @pl.when(edge_src & (h == borne))
        def _():
            pl.semaphore_wait(ready.at[0], 1)
            send_edge(h).start()

        @pl.when(helper & (h == jnp.minimum(jnp.maximum(z + 1, 3), heads - 1)))
        def _():
            pl.semaphore_wait(ready.at[0], 1)
            send_helper(z - 1).wait_recv()
            send_on().start()

        @pl.when(h < early)
        def _():
            part[h] = key_sum
            part[early + h] = val_sum

        @pl.when(h >= early)
        def _():
            late[pl.ds(h - early, 1)] = key_sum
            late[pl.ds(h, 1)] = val_sum

        return carry

    lax.fori_loop(0, heads, first_batch, 0)

    def send_part(d):
        to = lax.rem(dp + d, n_dp)
        return pltpu.make_async_remote_copy(
            src_ref=part.at[to], dst_ref=coll.at[dp],
            send_sem=one_s.at[d], recv_sem=one_r.at[d], device_id={"dp": to}, device_id_type=MESH,
        )

    def send_mid(k, d):
        return pltpu.make_async_remote_copy(
            src_ref=tot, dst_ref=mid.at[here, dp],
            send_sem=two_s.at[k, d], recv_sem=two_r.at[k, d],
            device_id=place(sides[k], None, lax.rem(dp + d, n_dp)), device_id_type=MESH,
        )

    def send_late(k, d):
        return pltpu.make_async_remote_copy(
            src_ref=late, dst_ref=gath.at[here, dp],
            send_sem=red_s.at[k, d], recv_sem=red_r.at[k, d],
            device_id=place(sides[k], None, lax.rem(dp + d, n_dp)), device_id_type=MESH,
        )

    order = [(k, d) for d in (4, 3, 5, 2, 6, 1, 7, 0) for k in range(2)]

    def second_batch(h, carry):
        for k in range(2):
            send_x(1, k, h).wait_send()

            @pl.when(h + 2 * LOOK < heads)
            def _():
                send_x(1, k, h + 2 * LOOK).start()

        for k in range(2):
            send_x(1, k, h).wait_recv()

        @pl.when(is_top)
        def _():
            own_u(h).wait()
            send_u(h).wait_recv()

        @pl.when(work < segments - 1)
        def _():
            send_down(h).wait_recv()

        x = jnp.concatenate([x_in[1, 0, h], x_in[1, 1, h]], axis=0)
        key_sum, val_sum, _ = head_math(
            x, arr[h], meta_in[pl.ds(h, 1)], meta_in[pl.ds(heads + h, 1)], bias_of(1), False
        )

        @pl.when(h < early)
        def _():
            part[h] += key_sum
            part[early + h] += val_sum

        @pl.when(h >= early)
        def _():
            late[pl.ds(h - early, 1)] += key_sum
            late[pl.ds(h, 1)] += val_sum

        @pl.when(h == early - 1)
        def _():
            @pl.when(later > 0)
            def _():
                pl.semaphore_wait(ready.at[2], later)

            coll[dp] = part[dp]
            for d in range(1, n_dp):
                send_part(d).start()

        @pl.when(h == heads - 2)
        def _():
            for d in range(1, n_dp):
                send_part(d).wait_recv()
            total = coll[0]
            for d in range(1, n_dp):
                total = total + coll[d]
            tot[...] = total
            for k, d in order:
                send_mid(k, d).start()

        return carry

    lax.fori_loop(0, heads, second_batch, 0)

    for k, d in order:
        send_late(k, d).start()
    for k, d in order:
        send_mid(k, d).wait_recv()
    for k, d in order:
        send_late(k, d).wait_recv()
    for s in range(2):
        total = gath[s, 0]
        for d in range(1, n_dp):
            total = total + gath[s, d]
        for h in range(heads):
            cols = slice((s * heads + h) * HEAD_DIM, (s * heads + h + 1) * HEAD_DIM)
            if h < early:
                key_sum = mid[s, h]
                val_sum = mid[s, early + h]
            else:
                key_sum = total[h - early : h - early + 1]
                val_sum = total[h : h + 1]
            out_ref[0, 0:1, cols] = sfv[1:2, cols] * key_sum
            out_ref[0, 1:2, cols] = sfv[0:1, cols] * key_sum
            out_ref[0, 2:3, cols] = sfv[3:4, cols] * val_sum
            out_ref[0, 3:4, cols] = sfv[2:3, cols] * val_sum

    def drain_down(h, carry):
        @pl.when(plain_src | edge_src)
        def _():
            send_down(h).wait_send()

        @pl.when(lender & (h == heads - 1 - z))
        def _():
            send_u(h).wait_send()

        return carry

    lax.fori_loop(0, heads, drain_down, 0)

    @pl.when(helper)
    def _():
        send_on().wait_send()

    send_meta().wait_send()
    for d in range(1, n_dp):
        send_part(d).wait_send()
    for k, d in order:
        send_mid(k, d).wait_send()
        send_late(k, d).wait_send()


def shards(segments, n_dp, x, pend, top, gains, table, count):
    rows, channels = x.shape[3], x.shape[4]
    heads = channels // HEAD_DIM // 2
    in_place = pl.BlockSpec(memory_space=pltpu.HBM)
    dma = pltpu.SemaphoreType.DMA
    low = jnp.bfloat16
    return pl.pallas_call(
        functools.partial(sweep_kernel, segments, n_dp, heads),
        out_shape=jax.ShapeDtypeStruct((1, 4, channels), jnp.float32),
        in_specs=[in_place] * 6,
        out_specs=pl.BlockSpec(memory_space=pltpu.VMEM),
        scratch_shapes=[
            pltpu.VMEM((2, 2, heads, rows, HEAD_DIM), low),
            pltpu.VMEM((2, heads, rows, HEAD_DIM), low),
            pltpu.VMEM((heads, 2 * rows, HEAD_DIM), low),
            pltpu.VMEM((heads, 2 * rows, HEAD_DIM), low),
            pltpu.VMEM((2 * rows, HEAD_DIM), low),
            pltpu.VMEM((4, channels), jnp.float32),
            pltpu.VMEM((2 * heads + 8, HEAD_DIM), jnp.float32),
            pltpu.VMEM((2 * heads + 8, HEAD_DIM), jnp.float32),
            pltpu.VMEM((n_dp, 1, HEAD_DIM), jnp.float32),
            pltpu.VMEM((heads, HEAD_DIM), jnp.float32),
            pltpu.VMEM((n_dp, 1, HEAD_DIM), jnp.float32),
            pltpu.VMEM((1, HEAD_DIM), jnp.float32),
            pltpu.VMEM((2, n_dp, 1, HEAD_DIM), jnp.float32),
            pltpu.VMEM((2, n_dp, heads, HEAD_DIM), jnp.float32),
            pltpu.SMEM((2, 2, 2), jnp.int32),
            pltpu.SMEM((2, 2), jnp.int32),
            dma((3 + heads,)),
            dma((2, 2, heads)),
            dma((2, 2, heads)),
            dma((2, heads)),
            dma((2, heads)),
            dma((1,)),
            dma((1,)),
            dma((heads,)),
            dma((heads,)),
            dma((heads,)),
            dma((1,)),
            dma((1,)),
            dma((n_dp,)),
            dma((n_dp,)),
            dma((2, n_dp)),
            dma((2, n_dp)),
            dma((2, n_dp)),
            dma((2, n_dp)),
            pltpu.SemaphoreType.REGULAR((3 + HELPERS,)),
        ],
        compiler_params=pltpu.CompilerParams(
            collective_id=1, has_side_effects=True, vmem_limit_bytes=32 << 20
        ),
        name="sweep",
    )(*[pltpu.with_memory_space_constraint(v, pltpu.HBM) for v in (x, pend, top, gains, table, count)])


def solution(mesh):
    placed = (
        P("segment", None, "dp", "seq", None),
        P("segment", "dp", "seq", None),
        P(None, "dp", "seq", None),
        P("segment", None, None),
        P("segment", None, "dp", None, None),
        P("segment", None, "dp", None),
    )
    body = functools.partial(shards, mesh.shape["segment"], mesh.shape["dp"])
    return jax.shard_map(
        body, mesh=mesh, in_specs=placed, out_specs=P("segment", None, None), check_vma=False
    )
```

time: 59.8 us -> 56.6 us (0.946)
  Pallas kernels: 59 us -> 55.8 us
    pallas_call x1, Pallas kernels: 59 us -> 55.8 us  [shards(): pl.pallas_call(functools.partial(sweep_kernel, segments, n_dp, heads), ou...]
where the time goes in v4:
time: 56.6 us; the launch traced here: 56.4 us
  Pallas kernels  55.8 us (99%)
  local copies, waits for them, and re-layouts  0.62 us (1%)
    pallas_call x1, Pallas kernels, shards(): pl.pallas_call(functools.partial(sweep_kernel, segments, n_dp, heads), ou...  55.8 us

profile of v4, /device:TPU:1, one launch (start us, length us, event | category | flops | bytes accessed | tf_op | source)
XLA Modules:
  0.0 56.4 jit_solution(14077597402960723364)
XLA Ops:
  0.0 55.8 %sweep.1 = f32[1,4,2048]{2,1,0:T(4,128)S(1)} custom-call(bf16[1,2,1,128,2048]{4,3,2,1,0:T(8,128)(2,1)} %x_ref.1, bf16[1,1,128,2048]{3,2,1,0:T(8,128)(2,1)} %p_ref.1, bf16[1,1,128,2048]{3,2,1,0:T(8,128)(2,1)} %u_ref.1, f32[1,4,2048]{2,1,0:T(4,128)} %sf_ref.1, s32[1,2,1,2,2]{4,3,2,1,0:T(2,128)} %tab_ref.1, s32[1,2,1,2]{3,2,1,0:T(1,128)} %cnt_ref.1), custom_call_target="tpu_custom_call" | custom-call | tf_op jit(solution)/shard_map/sweep/pallas_call | solution.py:501
  55.8 0.6 %copy.8 = f32[1,4,2048]{2,1,0:T(4,128)} copy(f32[1,4,2048]{2,1,0:T(4,128)S(1)} %sweep.1) | data formatting | bytes 65536

commit v5 on v4

--- a/solution.py
+++ b/solution.py
@@ -144,12 +144,16 @@
     def _():
         signal(barrier, top_at)
 
+    back = jnp.where(z == 0, 1, 0)
+    line = lax.rem(y + ring - back, ring)
+    turn = lax.rem(dp + n_dp - back, n_dp)
+
     def greet(t, carry):
-        signal(barrier, place(0, None, t))
+        signal(barrier, place(0, None, lax.rem(t + back, n_dp)))
         return carry
 
-    lax.fori_loop(dp + 1, n_dp, greet, 0)
-    higher = [lax.rem(y + dy + ring, ring) > y for dy in sides]
+    lax.fori_loop(turn + 1, n_dp, greet, 0)
+    higher = [lax.rem(line + dy + ring, ring) > line for dy in sides]
     for dy, up in zip(sides, higher):
         @pl.when(up)
         def _():
@@ -161,7 +165,7 @@
 
     pl.semaphore_wait(
         barrier,
-        2 + dp + sum(one(~up, n_dp - 1) for up in higher) + one(plain_src)
+        2 + turn + sum(one(~up, n_dp - 1) for up in higher) + one(plain_src)
         + one(edge_dst, 1 + HELPERS) + one(helper) + one(is_top, LENDERS),
     )
 
@@ -265,17 +269,17 @@
             signal(ready.at[1], {"segment": segments - RUN + k, "seq": 1 - seq})
 
     def answer(t, carry):
-        signal(ready.at[2], place(0, None, t))
+        signal(ready.at[2], place(0, None, lax.rem(t + back, n_dp)))
         return carry
 
-    lax.fori_loop(0, dp, answer, 0)
+    lax.fori_loop(0, turn, answer, 0)
     for dy, up in zip(sides, higher):
         @pl.when(~up)
         def _():
             for d in range(1, n_dp):
                 signal(ready.at[2], place(dy, None, lax.rem(dp + d, n_dp)))
 
-    later = n_dp - 1 - dp + sum(one(up, n_dp - 1) for up in higher)
+    later = n_dp - 1 - turn + sum(one(up, n_dp - 1) for up in higher)
 
     def bias_of(w):
         rows = []
@@ -341,7 +345,7 @@
             pl.semaphore_wait(ready.at[0], 1)
             send_edge(h).start()
 
-        @pl.when(helper & (h == jnp.minimum(jnp.maximum(z + 1, 3), heads - 1)))
+        @pl.when(helper & (h == jnp.minimum(jnp.maximum(z + 1, 5), heads - 1)))
         def _():
             pl.semaphore_wait(ready.at[0], 1)
             send_helper(z - 1).wait_recv()
@@ -429,43 +433,40 @@
             for d in range(1, n_dp):
                 send_part(d).start()
 
-        @pl.when(h == heads - 2)
-        def _():
-            for d in range(1, n_dp):
-                send_part(d).wait_recv()
-            total = coll[0]
-            for d in range(1, n_dp):
-                total = total + coll[d]
-            tot[...] = total
-            for k, d in order:
-                send_mid(k, d).start()
-
         return carry
 
     lax.fori_loop(0, heads, second_batch, 0)
 
     for k, d in order:
         send_late(k, d).start()
+    for d in range(1, n_dp):
+        send_part(d).wait_recv()
+    total = coll[0]
+    for d in range(1, n_dp):
+        total = total + coll[d]
+    tot[...] = total
     for k, d in order:
-        send_mid(k, d).wait_recv()
+        send_mid(k, d).start()
+    def write(s, h, key_sum, val_sum):
+        cols = slice((s * heads + h) * HEAD_DIM, (s * heads + h + 1) * HEAD_DIM)
+        out_ref[0, 0:1, cols] = sfv[1:2, cols] * key_sum
+        out_ref[0, 1:2, cols] = sfv[0:1, cols] * key_sum
+        out_ref[0, 2:3, cols] = sfv[3:4, cols] * val_sum
+        out_ref[0, 3:4, cols] = sfv[2:3, cols] * val_sum
+
     for k, d in order:
         send_late(k, d).wait_recv()
     for s in range(2):
         total = gath[s, 0]
         for d in range(1, n_dp):
             total = total + gath[s, d]
-        for h in range(heads):
-            cols = slice((s * heads + h) * HEAD_DIM, (s * heads + h + 1) * HEAD_DIM)
-            if h < early:
-                key_sum = mid[s, h]
-                val_sum = mid[s, early + h]
-            else:
-                key_sum = total[h - early : h - early + 1]
-                val_sum = total[h : h + 1]
-            out_ref[0, 0:1, cols] = sfv[1:2, cols] * key_sum
-            out_ref[0, 1:2, cols] = sfv[0:1, cols] * key_sum
-            out_ref[0, 2:3, cols] = sfv[3:4, cols] * val_sum
-            out_ref[0, 3:4, cols] = sfv[2:3, cols] * val_sum
+        for h in range(early, heads):
+            write(s, h, total[h - early : h - early + 1], total[h : h + 1])
+    for k, d in order:
+        send_mid(k, d).wait_recv()
+    for s in range(2):
+        for h in range(early):
+            write(s, h, mid[s, h], mid[s, early + h])
 
     def drain_down(h, carry):
         @pl.when(plain_src | edge_src)

time: 56.6 us -> 55.8 us (0.986)
  Pallas kernels: 55.8 us -> 54.8 us
    pallas_call x1, Pallas kernels: 55.8 us -> 54.8 us  [shards(): pl.pallas_call(functools.partial(sweep_kernel, segments, n_dp, heads), ou...]
where the time goes in v5:
time: 55.8 us; the launch traced here: 55.4 us
  Pallas kernels  54.8 us (98%)
  local copies, waits for them, and re-layouts  0.62 us (1%)
    pallas_call x1, Pallas kernels, shards(): pl.pallas_call(functools.partial(sweep_kernel, segments, n_dp, heads), ou...  54.8 us

profile of v5, /device:TPU:1, one launch (start us, length us, event | category | flops | bytes accessed | tf_op | source)
XLA Modules:
  0.0 55.4 jit_solution(5778838930024116912)
XLA Ops:
  0.0 54.8 %sweep.1 = f32[1,4,2048]{2,1,0:T(4,128)S(1)} custom-call(bf16[1,2,1,128,2048]{4,3,2,1,0:T(8,128)(2,1)} %x_ref.1, bf16[1,1,128,2048]{3,2,1,0:T(8,128)(2,1)} %p_ref.1, bf16[1,1,128,2048]{3,2,1,0:T(8,128)(2,1)} %u_ref.1, f32[1,4,2048]{2,1,0:T(4,128)} %sf_ref.1, s32[1,2,1,2,2]{4,3,2,1,0:T(2,128)} %tab_ref.1, s32[1,2,1,2]{3,2,1,0:T(1,128)} %cnt_ref.1), custom_call_target="tpu_custom_call" | custom-call | tf_op jit(solution)/shard_map/sweep/pallas_call | solution.py:502
  54.8 0.6 %copy.8 = f32[1,4,2048]{2,1,0:T(4,128)} copy(f32[1,4,2048]{2,1,0:T(4,128)S(1)} %sweep.1) | data formatting | bytes 65536

commit v6 on v5

--- a/solution.py
+++ b/solution.py
@@ -390,13 +390,6 @@
 
     def second_batch(h, carry):
         for k in range(2):
-            send_x(1, k, h).wait_send()
-
-            @pl.when(h + 2 * LOOK < heads)
-            def _():
-                send_x(1, k, h + 2 * LOOK).start()
-
-        for k in range(2):
             send_x(1, k, h).wait_recv()
 
         @pl.when(is_top)
@@ -469,6 +462,9 @@
             write(s, h, mid[s, h], mid[s, early + h])
 
     def drain_down(h, carry):
+        for k in range(2):
+            send_x(1, k, h).wait_send()
+
         @pl.when(plain_src | edge_src)
         def _():
             send_down(h).wait_send()

time: 55.8 us -> 55.8 us (level)
  no operation moved by 1% of the time
where the time goes in v6:
time: 55.8 us; the launch traced here: 55.4 us
  Pallas kernels  54.8 us (98%)
  local copies, waits for them, and re-layouts  0.62 us (1%)
    pallas_call x1, Pallas kernels, shards(): pl.pallas_call(functools.partial(sweep_kernel, segments, n_dp, heads), ou...  54.8 us

profile of v6, /device:TPU:1, one launch (start us, length us, event | category | flops | bytes accessed | tf_op | source)
XLA Modules:
  0.0 55.4 jit_solution(15121012326434761386)
XLA Ops:
  0.0 54.8 %sweep.1 = f32[1,4,2048]{2,1,0:T(4,128)S(1)} custom-call(bf16[1,2,1,128,2048]{4,3,2,1,0:T(8,128)(2,1)} %x_ref.1, bf16[1,1,128,2048]{3,2,1,0:T(8,128)(2,1)} %p_ref.1, bf16[1,1,128,2048]{3,2,1,0:T(8,128)(2,1)} %u_ref.1, f32[1,4,2048]{2,1,0:T(4,128)} %sf_ref.1, s32[1,2,1,2,2]{4,3,2,1,0:T(2,128)} %tab_ref.1, s32[1,2,1,2]{3,2,1,0:T(1,128)} %cnt_ref.1), custom_call_target="tpu_custom_call" | custom-call | tf_op jit(solution)/shard_map/sweep/pallas_call | solution.py:498
  54.8 0.6 %copy.8 = f32[1,4,2048]{2,1,0:T(4,128)} copy(f32[1,4,2048]{2,1,0:T(4,128)S(1)} %sweep.1) | data formatting | bytes 65536
